TPU v7x, 32 devices: a whole 2x2x4 slice. The times are simulated.
32 devices in a mesh: groups: 2 (over y), lon: 4 (over z), lat: 2 (over x), segment: 2 (over core).
Axes of the slice: x: 2, y: 2, z: 4, core: 2. Of those that a mesh axis runs over, the one named last changes fastest.
Arguments:
- inputs: bfloat16 [32, 128, 512], P(('groups', 'lat'), 'lon'), parts along dimension 0, may hold values from -6 to 6
- cotangent: bfloat16 [32, 128, 512], P(('groups', 'lat'), 'lon'), parts along dimension 0, may hold values from -8 to 8
- kernel: bfloat16 [2, 49, 512], P('segment'), may hold values from -0.875 to 0.875
- conv_bias: float32 [2, 512], P('segment'), may hold values from -3 to 3
- norm_gain: float32 [2, 512], P('segment'), may hold values from 0.5 to 2
- norm_shift: float32 [2, 512], P('segment'), may hold values from -3 to 3
- up_weight: bfloat16 [2, 512, 2048], P('segment'), may hold values from -0.25 to 0.25
- hidden_bias: float32 [2, 2048], P('segment'), may hold values from -3 to 3
- down_weight: bfloat16 [2, 2048, 512], P('segment'), may hold values from -0.125 to 0.125
- out_bias: float32 [2, 512], P('segment'), may hold values from -3 to 3
- layer_scale: float32 [2, 512], P('segment'), may hold values from 0.5 to 1.5
Outputs:
- section_out: bfloat16 [2, 32, 128, 512], P('segment', ('groups', 'lat'), 'lon'), parts along dimension 1
- boundary_grad: bfloat16 [2, 32, 128, 512], P('segment', ('groups', 'lat'), 'lon'), parts along dimension 1
- up_grad: float32 [4, 512, 2048], P(('groups', 'segment'), None, ('lon', 'lat')), parts along dimension 0
- down_grad: float32 [4, 2048, 512], P(('groups', 'segment'), ('lon', 'lat')), parts along dimension 0
- hidden_bias_grad: float32 [4, 2048], P(('groups', 'segment'), ('lon', 'lat')), parts along dimension 0
- kernel_grad: float32 [4, 49, 512], P(('groups', 'segment'), None, ('lon', 'lat')), parts along dimension 0
- vector_grad: float32 [4, 5, 512], P(('groups', 'segment'), None, ('lon', 'lat')), parts along dimension 0
There are 2 independent parts, one for each index of `groups`. A program takes and returns all parts, laid end to end along the dimension named above; an argument that names none is the same for every part. Nothing has to cross between parts.
All inputs are finite; a program needn't handle non-finite values.
Results may differ from a plain program's by a relative error of at most 0.023.
Values may be sent and summed in bfloat16 or wider, within the bound.
A program may use at most 128 MiB of HBM per device.

v0:
```python
import jax
import jax.numpy as jnp
from jax import lax
from jax.sharding import PartitionSpec as P

KERNEL = 7


EPSILON = 1e-06
ROOT_HALF = 0.7071067811865476
DENSITY_SCALE = 0.3989422804014327


def extended(cells, sides, width, closed):
    for axis, dim in sides:
        count = lax.axis_size(axis)
        ends = count if closed else count - 1
        head = lax.slice_in_dim(cells, 0, width, axis=dim)
        tail = lax.slice_in_dim(cells, cells.shape[dim] - width, cells.shape[dim], axis=dim)
        cells = jnp.concatenate(
            [
                lax.ppermute(tail, axis, [(i, (i + 1) % count) for i in range(ends)]),
                cells,
                lax.ppermute(head, axis, [((i + 1) % count, i) for i in range(ends)]),
            ],
            axis=dim,
        )
    return cells


def from_behind(value, axis, steps):
    count = lax.axis_size(axis)
    pairs = [(source, (source + steps) % count) for source in range(count)]
    return lax.ppermute(value, axis, pairs)


def partner_2(shard, axis, apart):
    return lax.ppermute(shard, axis, [(i, i ^ 1 << apart) for i in range(lax.axis_size(axis))])


def correlate(padded, stencil, out_rows, out_cols):
    accumulated = jnp.zeros((out_rows, out_cols, padded.shape[2]), jnp.float32)
    for row_tap in range(KERNEL):
        for col_tap in range(KERNEL):
            window = padded[row_tap : row_tap + out_rows, col_tap : col_tap + out_cols].astype(
                jnp.float32
            )
            accumulated = accumulated + window * stencil[row_tap, col_tap].astype(jnp.float32)
    return accumulated


def stencil_terms(padded, grad_low, out_rows, out_cols):
    grad_wide = grad_low.astype(jnp.float32)
    columns = []
    for row_tap in range(KERNEL):
        for col_tap in range(KERNEL):
            window = padded[row_tap : row_tap + out_rows, col_tap : col_tap + out_cols].astype(
                jnp.float32
            )
            columns.append(jnp.sum(window * grad_wide, axis=(0, 1)))
    return jnp.stack(columns)


def gelu_parts(before):
    cumulative = 0.5 * (1.0 + lax.erf(before * ROOT_HALF))
    density = jnp.exp(-0.5 * before * before) * DENSITY_SCALE
    return (before * cumulative, cumulative + before * density)


def forward_section(values, padded, params):
    (
        stencil,
        conv_bias,
        norm_gain,
        norm_shift,
        up_matrix,
        bias_hidden,
        down_matrix,
        bias_out,
        scaling,
    ) = params
    out_rows, out_cols, channels = values.shape
    stencil_grid = stencil.reshape(KERNEL, KERNEL, channels)
    activity = correlate(padded, stencil_grid, out_rows, out_cols) + conv_bias
    average = jnp.mean(activity, axis=-1, keepdims=True)
    centred = activity - average
    variance = jnp.mean(centred * centred, axis=-1, keepdims=True)
    inverse = lax.rsqrt(variance + EPSILON)
    unit_norm = centred * inverse
    normed = (
        (unit_norm * norm_gain + norm_shift)
        .astype(jnp.bfloat16)
        .reshape(out_rows * out_cols, channels)
    )
    before = jnp.dot(normed, up_matrix, preferred_element_type=jnp.float32) + bias_hidden
    activated, slope_value = gelu_parts(before)
    hidden = activated.astype(jnp.bfloat16)
    branch = jnp.dot(hidden, down_matrix, preferred_element_type=jnp.float32) + bias_out
    result = (
        values.astype(jnp.float32) + scaling * branch.reshape(out_rows, out_cols, channels)
    ).astype(jnp.bfloat16)
    return (result, (padded, unit_norm, inverse, normed, slope_value, hidden, branch))


def backward_section(stored, upstream, params, extender, north_weight, south_weight):
    padded, unit_norm, inverse, normed, slope_value, hidden, branch = stored
    (
        stencil,
        conv_bias,
        norm_gain,
        norm_shift,
        up_matrix,
        bias_hidden,
        down_matrix,
        bias_out,
        scaling,
    ) = params
    out_rows, out_cols, channels = upstream.shape
    margin = KERNEL // 2
    incoming = upstream.astype(jnp.float32)
    incoming_flat = incoming.reshape(out_rows * out_cols, channels)
    scale_grad = jnp.sum(incoming_flat * branch, axis=0)
    scaled = (incoming_flat * scaling).astype(jnp.bfloat16)
    bias_out_grad = jnp.sum(scaled.astype(jnp.float32), axis=0)
    down_sum = jnp.dot(hidden.T, scaled, preferred_element_type=jnp.float32)
    hidden_grad = jnp.dot(scaled, down_matrix.T, preferred_element_type=jnp.float32)
    before_grad = (hidden_grad * slope_value).astype(jnp.bfloat16)
    up_sum = jnp.dot(normed.T, before_grad, preferred_element_type=jnp.float32)
    bias_sum = jnp.sum(before_grad.astype(jnp.float32), axis=0)
    normed_grad = jnp.dot(before_grad, up_matrix.T, preferred_element_type=jnp.float32).reshape(
        out_rows, out_cols, channels
    )
    gain_grad = jnp.sum(normed_grad * unit_norm, axis=(0, 1))
    shift_grad = jnp.sum(normed_grad, axis=(0, 1))
    gained = normed_grad * norm_gain
    activity_grad = inverse * (
        gained
        - jnp.mean(gained, axis=-1, keepdims=True)
        - unit_norm * jnp.mean(gained * unit_norm, axis=-1, keepdims=True)
    )
    activity_low = activity_grad.astype(jnp.bfloat16)
    conv_bias_grad = jnp.sum(activity_low.astype(jnp.float32), axis=(0, 1))
    stencil_sum = stencil_terms(padded, activity_low, out_rows, out_cols)
    spread = extender(activity_low)
    stencil_grid = stencil.reshape(KERNEL, KERNEL, channels).astype(jnp.float32)
    flipped = stencil_grid[::-1, ::-1]
    correction = stencil_grid[:, ::-1] - flipped
    through = correlate(spread, flipped, out_rows, out_cols)
    zero_rows = jnp.zeros_like(spread[: 2 * margin])
    top_part = jnp.concatenate([spread[:margin], zero_rows], axis=0)
    bottom_part = jnp.concatenate([zero_rows, spread[-margin:]], axis=0)
    top_fix = correlate(top_part, correction, margin, out_cols) * north_weight
    bottom_fix = correlate(bottom_part, correction, margin, out_cols) * south_weight
    rest_rows = out_rows - margin
    top_full = jnp.pad(top_fix, ((0, rest_rows), (0, 0), (0, 0)))
    bottom_full = jnp.pad(bottom_fix, ((rest_rows, 0), (0, 0), (0, 0)))
    through = through + top_full + bottom_full
    passed = (incoming + through).astype(jnp.bfloat16)
    vectors = jnp.stack([conv_bias_grad, gain_grad, shift_grad, bias_out_grad, scale_grad])
    return (passed, (up_sum, down_sum, bias_sum, stencil_sum, vectors))


def lat_neighbours(edge_rows):
    return extended(edge_rows, (("lat", 0),), KERNEL // 2, False)


CYCLE = ("lon", "segment")


def lon_neighbours(edge_cols):
    return extended(edge_cols, ((CYCLE, 1),), KERNEL // 2, True)


def pole_partner(edge_rows):
    return from_behind(edge_rows, CYCLE, lax.axis_size(CYCLE) // 2)


def hand_over(values):
    return partner_2(values, "segment", 0)


def extend_local(values, northern, southern, row_source):
    margin = KERNEL // 2
    edge_rows = jnp.concatenate([values[:margin], values[-margin:]], axis=0)
    nearby = row_source(edge_rows)
    partner = pole_partner(edge_rows)
    upper_rows = jnp.where(northern, partner[:margin][::-1], nearby[:margin])
    lower_rows = jnp.where(southern, partner[margin:][::-1], nearby[-margin:])
    lat_extended = jnp.concatenate([upper_rows, values, lower_rows], axis=0)
    edge_cols = jnp.concatenate([lat_extended[:, :margin], lat_extended[:, -margin:]], axis=1)
    beside_all = lon_neighbours(edge_cols)
    return jnp.concatenate([beside_all[:, :margin], lat_extended, beside_all[:, -margin:]], axis=1)


def both_halves(leading, first, second, dim):
    received = hand_over(jnp.where(leading, second, first))
    own = jnp.where(leading, first, second)
    return jnp.where(
        leading,
        jnp.concatenate([own, received], axis=dim),
        jnp.concatenate([received, own], axis=dim),
    )


def scattered(value, dim):
    return lax.psum_scatter(
        value.astype(jnp.bfloat16), ("lon", "lat", "segment"), scatter_dimension=dim, tiled=True
    )


def packed(sums):
    _, _, bias_sum, stencil_sum, vectors = sums
    channels = vectors.shape[1]
    pieces = lax.axis_size(("lon", "lat"))
    bias_rows = (
        bias_sum.reshape(pieces, -1, channels // pieces).transpose(1, 0, 2).reshape(-1, channels)
    )
    return jnp.concatenate([stencil_sum, vectors, bias_rows], axis=0)


def local(
    inputs,
    cotangent,
    kernel,
    conv_bias,
    norm_gain,
    norm_shift,
    up_weight,
    hidden_bias,
    down_weight,
    out_bias,
    layer_scale,
):
    core = lax.axis_index("segment")
    leading = core == 0
    width = inputs.shape[1] // lax.axis_size("segment")
    channels = inputs.shape[2]
    inputs = lax.dynamic_slice_in_dim(inputs, core * width, width, axis=1)
    cotangent = lax.dynamic_slice_in_dim(cotangent, core * width, width, axis=1)
    rows = jnp.concatenate(
        [conv_bias, norm_gain, norm_shift, out_bias, layer_scale, hidden_bias.reshape(-1, channels)],
        axis=0,
    )
    taps, rows, ups, downs = [
        lax.all_gather(value, "segment", axis=0)
        for value in (kernel[0], rows, up_weight[0], down_weight[0])
    ]
    sections = [
        (
            taps[s],
            rows[s, 0],
            rows[s, 1],
            rows[s, 2],
            ups[s],
            rows[s, 5:].reshape(-1),
            downs[s],
            rows[s, 3],
            rows[s, 4],
        )
        for s in range(2)
    ]
    northern = lax.axis_index("lat") == 0
    southern = lax.axis_index("lat") == lax.axis_size("lat") - 1
    north_weight = jnp.where(northern, 1.0, 0.0).astype(jnp.float32)
    south_weight = jnp.where(southern, 1.0, 0.0).astype(jnp.float32)

    def extender(values):
        return extend_local(values, northern, southern, lat_neighbours)

    first_out, first_stored = forward_section(inputs, extender(inputs), sections[0])
    second_out, second_stored = forward_section(first_out, extender(first_out), sections[1])
    second_grad, second_sums = backward_section(
        second_stored, cotangent, sections[1], extender, north_weight, south_weight
    )
    up_second = scattered(second_sums[0], 1)
    down_second = scattered(second_sums[1], 0)
    first_grad, first_sums = backward_section(
        first_stored, second_grad, sections[0], extender, north_weight, south_weight
    )
    up_first = scattered(first_sums[0], 1)
    down_first = scattered(first_sums[1], 0)
    section_out = both_halves(leading, first_out, second_out, 1)[None]
    boundary_grad = both_halves(leading, first_grad, second_grad, 1)[None]
    up_part = both_halves(leading, up_first, up_second, 1).astype(jnp.float32)
    down_part = both_halves(leading, down_first, down_second, 0).astype(jnp.float32)
    first_small = packed(first_sums)
    second_small = packed(second_sums)
    small = jnp.where(leading, first_small, second_small) + hand_over(
        jnp.where(leading, second_small, first_small)
    )
    small = lax.psum_scatter(
        small.astype(jnp.bfloat16), ("lon", "lat"), scatter_dimension=1, tiled=True
    ).astype(jnp.float32)
    count = KERNEL * KERNEL
    stencil_part = small[:count]
    vector_part = small[count : count + 5]
    bias_part = small[count + 5 :].reshape(-1)
    return (
        section_out,
        boundary_grad,
        up_part[None],
        down_part[None],
        bias_part[None],
        stencil_part[None],
        vector_part[None],
    )


def solution(mesh):
    placed = (
        P(("groups", "lat"), "lon", None),
        P(("groups", "lat"), "lon", None),
        P("segment", None, None),
        P("segment", None),
        P("segment", None),
        P("segment", None),
        P("segment", None, None),
        P("segment", None),
        P("segment", None, None),
        P("segment", None),
        P("segment", None),
    )
    return jax.shard_map(
        local,
        mesh=mesh,
        in_specs=placed,
        out_specs=(
            P("segment", ("groups", "lat"), "lon", None),
            P("segment", ("groups", "lat"), "lon", None),
            P(("groups", "segment"), None, ("lon", "lat")),
            P(("groups", "segment"), ("lon", "lat"), None),
            P(("groups", "segment"), ("lon", "lat")),
            P(("groups", "segment"), None, ("lon", "lat")),
            P(("groups", "segment"), None, ("lon", "lat")),
        ),
        check_vma=False,
    )
```

profile of v0, /device:TPU:0, one launch (start us, length us, event | category | flops | bytes accessed | tf_op | source)
XLA Modules:
  0.0 437.7 jit_solution(7402040572963187896)
XLA Ops:
  8.1 1.3 collective-permute-start.2
  9.4 4.9 %collective-permute-start.1 = (bf16[3,16,512]{2,1,0:T(8,128)(2,1)S(1)}, bf16[3,16,512]{2,1,0:T(8,128)(2,1)S(1)}, u32[]{:S(2)}, u32[]{:S(2)}) collective-permute-start(bf16[3,16,512]{2,1,0:T(8,128)(2,1)S(1)} %get-tuple-element.171), channel_id=1, source_target_pairs={{0,2},{1,3},{4,6},{5,7},{8,10},{9,11},{12,14},{13,15},{16,18},{17,... | collective-permute-start | bytes 147464 | tf_op jit(solution)/shard_map/ppermute | solution.py:22
  14.3 3.8 collective-permute-start
  18.2 1.9 all_gather.17
  21.7 1.9 all-gather.1
  33.8 3.4 collective-permute-start.4
  37.8 1.8 collective-permute-done.3
  39.7 2.6 fusion.334
  42.7 3.2 multiply_convert_fusion.1
  45.9 2.2 fusion.15
  48.9 2.3 collective-permute-start.6
  51.2 1.3 collective-permute-start.7
  52.5 3.4 collective-permute-done.5
  56.0 1.2 collective-permute-done.7
  57.4 3.5 collective-permute-start.9
  61.4 1.5 collective-permute-done.8
  63.1 2.6 fusion.332
  66.8 1.6 copy-done.171
  68.4 1.5 convert_reduce_fusion.2
  69.9 1.5 multiply_reduce_fusion
  72.1 1.9 collective-permute-start.12
  74.0 1.3 collective-permute-start.13
  75.3 1.1 fusion.205
  76.5 1.8 fusion.285
  78.6 5.4 %collective-permute-done.11 = bf16[6,16,512]{2,1,0:T(8,128)(2,1)S(1)} collective-permute-done((bf16[6,16,512]{2,1,0:T(8,128)(2,1)S(1)}, bf16[6,16,512]{2,1,0:T(8,128)(2,1)S(1)}, u32[]{:S(2)}, u32[]{:S(2)}) %collective-permute-start.11) | collective-permute-done | bytes 98336 | tf_op jit(solution)/shard_map/ppermute | solution.py:34
  84.3 3.5 collective-permute-start.15
  88.5 3.7 concatenate.445
  92.4 0.7 slice_select_fusion.1
  93.4 0.9 add_multiply_fusion.4
  94.6 1.2 add_multiply_fusion.5
  96.0 3.6 fusion.289
  99.6 0.9 convert_reduce_fusion.3
  100.5 1.5 copy-done.170
  102.0 1.0 multiply_reduce_fusion.1
  105.4 1.3 collective-permute-done.24
  106.7 0.8 copy.30
  107.6 1.8 convolution_convert_fusion.2
  109.3 2.5 copy.28
  111.9 1.0 copy-done.3
  112.9 2.0 convolution_convert_fusion
  118.7 2.1 convolution_convert_fusion.1
  129.7 4.3 collective-permute-start.17
  134.0 1.3 collective-permute-start.18
  135.3 2.5 copy.26
  137.9 0.8 fusion.346
  138.7 1.3 collective-permute-done.18
  140.3 3.5 collective-permute-start.20
  143.9 0.8 maximum_select_fusion
  144.9 1.3 collective-permute-done.19
  146.7 0.9 add_multiply_fusion.2
  148.6 1.2 add_multiply_fusion.3
  150.0 3.3 select_bitcast_fusion.2
  153.8 15.6 %reduce-scatter.20.cloned.1.call-done = bf16[64,58]{1,0:T(8,128)(2,1)} async-done(((bf16[512,58]{1,0:T(8,128)(2,1)}), bf16[64,58]{1,0:T(8,128)(2,1)}) %reduce-scatter.20.cloned.1.call-update) | async-done | bytes 7440
  169.4 0.8 copy.31
  172.2 61.8 %reduce-scatter.18.cloned.1.call-done = bf16[128,512]{1,0:T(8,128)(2,1)} async-done(((bf16[2048,512]{1,0:T(8,128)(2,1)}), bf16[128,512]{1,0:T(8,128)(2,1)}) %reduce-scatter.18.cloned.1.call-update) | async-done | bytes 131088
  233.9 1.0 copy.29
  234.9 63.4 %reduce-scatter.14.cloned.1.call-done = bf16[128,512]{1,0:T(8,128)(2,1)} async-done(((bf16[2048,512]{1,0:T(8,128)(2,1)}), bf16[128,512]{1,0:T(8,128)(2,1)}) %reduce-scatter.14.cloned.1.call-update) | async-done | bytes 131088 | tf_op jit(solution)/shard_map/reduce_scatter | solution.py:206
  298.3 64.4 %reduce-scatter.12.cloned.1.call-done = bf16[128,512]{1,0:T(8,128)(2,1)} async-done(((bf16[2048,512]{1,0:T(8,128)(2,1)}), bf16[128,512]{1,0:T(8,128)(2,1)}) %reduce-scatter.12.cloned.1.call-update) | async-done | bytes 131088 | tf_op jit(solution)/shard_map/reduce_scatter | solution.py:206
  362.7 1.0 select_bitcast_fusion
  363.8 63.4 %reduce-scatter.16.cloned.1.call-done = bf16[128,512]{1,0:T(8,128)(2,1)} async-done(((bf16[2048,512]{1,0:T(8,128)(2,1)}), bf16[128,512]{1,0:T(8,128)(2,1)}) %reduce-scatter.16.cloned.1.call-update) | async-done | bytes 131088
  427.2 1.0 copy.27
  428.4 0.8 maximum_select_fusion.1
  429.1 0.9 fusion.281
  430.0 0.9 fusion.280
  (525 shorter events, 36.8 us)
Async XLA Ops:
  7.2 11.0 %copy-start.13 = (bf16[1,49,512]{2,1,0:T(8,128)(2,1)S(1)}, bf16[1,49,512]{2,1,0:T(8,128)(2,1)}, u32[]{:S(2)}) copy-start(bf16[1,49,512]{2,1,0:T(8,128)(2,1)} %param.13) | copy-start | bytes 150532
  7.2 35.5 %all-gather.5.cloned.1.call-start = ((), (), s32[]{:S(2)}) async-start(), calls=%async_computation.5 | async-start | bytes 6291456 | tf_op jit(solution)/shard_map/all_gather | solution.py:245
  7.9 12.9 %copy-start.162 = (f32[1,2048]{1,0:T(1,128)S(1)}, f32[1,2048]{1,0:T(1,128)}, u32[]{:S(2)}) copy-start(f32[1,2048]{1,0:T(1,128)} %param.18) | copy-start | bytes 24580
  7.9 13.5 %copy-start.163 = (f32[1,512]{1,0:T(1,128)S(1)}, f32[1,512]{1,0:T(1,128)}, u32[]{:S(2)}) copy-start(f32[1,512]{1,0:T(1,128)} %param.14) | copy-start | bytes 6148
  7.9 13.5 %copy-start.164 = (f32[1,512]{1,0:T(1,128)S(1)}, f32[1,512]{1,0:T(1,128)}, u32[]{:S(2)}) copy-start(f32[1,512]{1,0:T(1,128)} %param.15) | copy-start | bytes 6148
  8.0 13.5 %copy-start.165 = (f32[1,512]{1,0:T(1,128)S(1)}, f32[1,512]{1,0:T(1,128)}, u32[]{:S(2)}) copy-start(f32[1,512]{1,0:T(1,128)} %param.16) | copy-start | bytes 6148
  8.0 13.5 %copy-start.166 = (f32[1,512]{1,0:T(1,128)S(1)}, f32[1,512]{1,0:T(1,128)}, u32[]{:S(2)}) copy-start(f32[1,512]{1,0:T(1,128)} %param.20) | copy-start | bytes 6148
  8.0 13.5 %copy-start.167 = (f32[1,512]{1,0:T(1,128)S(1)}, f32[1,512]{1,0:T(1,128)}, u32[]{:S(2)}) copy-start(f32[1,512]{1,0:T(1,128)} %param.21) | copy-start | bytes 6148
  8.0 37.9 %all-gather.7.cloned.1.call-start = ((), (), s32[]{:S(2)}) async-start(), calls=%async_computation.6 | async-start | bytes 6291456 | tf_op jit(solution)/shard_map/all_gather | solution.py:245
  8.1 25.3 %collective-permute-start.2 = (bf16[3,16,512]{2,1,0:T(8,128)(2,1)S(1)}, bf16[3,16,512]{2,1,0:T(8,128)(2,1)S(1)}, u32[]{:S(2)}, u32[]{:S(2)}) collective-permute-start(bf16[3,16,512]{2,1,0:T(8,128)(2,1)S(1)} %get-tuple-element.172), channel_id=1, source_target_pairs={{2,0},{3,1},{6,4},{7,5},{10,8},{11,9},{14,12},{15,13},{18,16},{19,... | collective-permute-start | bytes 147464 | tf_op jit(solution)/shard_map/ppermute | solution.py:24
  9.4 24.1 %collective-permute-start.1 = (bf16[3,16,512]{2,1,0:T(8,128)(2,1)S(1)}, bf16[3,16,512]{2,1,0:T(8,128)(2,1)S(1)}, u32[]{:S(2)}, u32[]{:S(2)}) collective-permute-start(bf16[3,16,512]{2,1,0:T(8,128)(2,1)S(1)} %get-tuple-element.171), channel_id=1, source_target_pairs={{0,2},{1,3},{4,6},{5,7},{8,10},{9,11},{12,14},{13,15},{16,18},{17,... | collective-permute-start | bytes 147464 | tf_op jit(solution)/shard_map/ppermute | solution.py:22
  14.3 18.2 %copy-start.8 = (bf16[8,32,512]{2,1,0:T(8,128)(2,1)S(1)}, bf16[8,32,512]{2,1,0:T(8,128)(2,1)}, u32[]{:S(2)}) copy-start(bf16[8,32,512]{2,1,0:T(8,128)(2,1)} %param.12) | copy-start | bytes 786436
  14.3 19.1 %collective-permute-start = (bf16[6,16,512]{2,1,0:T(8,128)(2,1)S(1)}, bf16[6,16,512]{2,1,0:T(8,128)(2,1)S(1)}, u32[]{:S(2)}, u32[]{:S(2)}) collective-permute-start(bf16[6,16,512]{2,1,0:T(8,128)(2,1)S(1)} %pad_maximum_fusion.14), channel_id=1, source_target_pairs={{0,8},{1,9},{4,12},{5,13},{8,0},{9,1},{12,4},{13,5},{2,10},{3,11},... | collective-permute-start | bytes 294920 | tf_op jit(solution)/shard_map/ppermute | solution.py:34
  18.2 151.3 %reduce-scatter.20.cloned.1.call-start = ((), (), s32[]{:S(2)}) async-start(), calls=%async_computation.11 | async-start | bytes 147456
  24.8 17.5 %copy-start.14 = (f32[1,1,512]{2,1,0:T(1,128)}, f32[1,1,512]{2,1,0:T(1,128)S(1)}, u32[]{:S(2)}) copy-start(f32[1,1,512]{2,1,0:T(1,128)S(1)} %get-tuple-element.261) | copy-start | bytes 6148
  24.8 17.5 %copy-start.16 = (f32[1,1,512]{2,1,0:T(1,128)}, f32[1,1,512]{2,1,0:T(1,128)S(1)}, u32[]{:S(2)}) copy-start(f32[1,1,512]{2,1,0:T(1,128)S(1)} %get-tuple-element.262) | copy-start | bytes 6148
  31.9 16.4 %copy-start.18 = (f32[1,1,512]{2,1,0:T(1,128)}, f32[1,1,512]{2,1,0:T(1,128)S(1)}, u32[]{:S(2)}) copy-start(f32[1,1,512]{2,1,0:T(1,128)S(1)} %get-tuple-element.264) | copy-start | bytes 6148
  31.9 16.4 %copy-start.20 = (f32[1,1,512]{2,1,0:T(1,128)}, f32[1,1,512]{2,1,0:T(1,128)S(1)}, u32[]{:S(2)}) copy-start(f32[1,1,512]{2,1,0:T(1,128)S(1)} %get-tuple-element.265) | copy-start | bytes 6148
  33.6 6.0 %collective-permute-start.3 = (bf16[14,3,512]{2,1,0:T(4,128)(2,1)S(1)}, bf16[14,3,512]{2,1,0:T(4,128)(2,1)S(1)}, u32[]{:S(2)}, u32[]{:S(2)}) collective-permute-start(bf16[14,3,512]{2,1,0:T(4,128)(2,1)S(1)} %get-tuple-element.187), channel_id=1, source_target_pairs={{0,1},{1,4},{4,5},{5,8},{8,9},{9,12},{12,13},{13,0},{2,3},{3,6},{6... | collective-permute-start | bytes 129032 | tf_op jit(solution)/shard_map/ppermute | solution.py:22
  33.8 5.8 %collective-permute-start.4 = (bf16[14,3,512]{2,1,0:T(4,128)(2,1)S(1)}, bf16[14,3,512]{2,1,0:T(4,128)(2,1)S(1)}, u32[]{:S(2)}, u32[]{:S(2)}) collective-permute-start(bf16[14,3,512]{2,1,0:T(4,128)(2,1)S(1)} %get-tuple-element.188), channel_id=1, source_target_pairs={{1,0},{4,1},{5,4},{8,5},{9,8},{12,9},{13,12},{0,13},{3,2},{6,3},{7... | collective-permute-start | bytes 129032 | tf_op jit(solution)/shard_map/ppermute | solution.py:24
  48.2 7.7 %collective-permute-start.5 = (bf16[6,16,512]{2,1,0:T(8,128)(2,1)S(1)}, bf16[6,16,512]{2,1,0:T(8,128)(2,1)S(1)}, u32[]{:S(2)}, u32[]{:S(2)}) collective-permute-start(bf16[6,16,512]{2,1,0:T(8,128)(2,1)S(1)} %pad_maximum_fusion.15), channel_id=1, source_target_pairs={{0,8},{1,9},{4,12},{5,13},{8,0},{9,1},{12,4},{13,5},{2,10},{3,11},... | collective-permute-start | bytes 294920 | tf_op jit(solution)/shard_map/ppermute | solution.py:34
  48.9 7.0 %collective-permute-start.6 = (bf16[3,16,512]{2,1,0:T(8,128)(2,1)S(1)}, bf16[3,16,512]{2,1,0:T(8,128)(2,1)S(1)}, u32[]{:S(2)}, u32[]{:S(2)}) collective-permute-start(bf16[3,16,512]{2,1,0:T(8,128)(2,1)S(1)} %get-tuple-element.193), channel_id=1, source_target_pairs={{0,2},{1,3},{4,6},{5,7},{8,10},{9,11},{12,14},{13,15},{16,18},{17,... | collective-permute-start | bytes 147464 | tf_op jit(solution)/shard_map/ppermute | solution.py:22
  51.2 6.0 %collective-permute-start.7 = (bf16[3,16,512]{2,1,0:T(8,128)(2,1)S(1)}, bf16[3,16,512]{2,1,0:T(8,128)(2,1)S(1)}, u32[]{:S(2)}, u32[]{:S(2)}) collective-permute-start(bf16[3,16,512]{2,1,0:T(8,128)(2,1)S(1)} %get-tuple-element.194), channel_id=1, source_target_pairs={{2,0},{3,1},{6,4},{7,5},{10,8},{11,9},{14,12},{15,13},{18,16},{19,... | collective-permute-start | bytes 147464 | tf_op jit(solution)/shard_map/ppermute | solution.py:24
  57.3 5.6 %collective-permute-start.8 = (bf16[14,3,512]{2,1,0:T(4,128)(2,1)S(1)}, bf16[14,3,512]{2,1,0:T(4,128)(2,1)S(1)}, u32[]{:S(2)}, u32[]{:S(2)}) collective-permute-start(bf16[14,3,512]{2,1,0:T(4,128)(2,1)S(1)} %get-tuple-element.183), channel_id=1, source_target_pairs={{0,1},{1,4},{4,5},{5,8},{8,9},{9,12},{12,13},{13,0},{2,3},{3,6},{6... | collective-permute-start | bytes 129032 | tf_op jit(solution)/shard_map/ppermute | solution.py:22
  57.4 5.5 %collective-permute-start.9 = (bf16[14,3,512]{2,1,0:T(4,128)(2,1)S(1)}, bf16[14,3,512]{2,1,0:T(4,128)(2,1)S(1)}, u32[]{:S(2)}, u32[]{:S(2)}) collective-permute-start(bf16[14,3,512]{2,1,0:T(4,128)(2,1)S(1)} %get-tuple-element.184), channel_id=1, source_target_pairs={{1,0},{4,1},{5,4},{8,5},{9,8},{12,9},{13,12},{0,13},{3,2},{6,3},{7... | collective-permute-start | bytes 129032 | tf_op jit(solution)/shard_map/ppermute | solution.py:24
  72.1 11.9 %collective-permute-start.12 = (bf16[3,16,512]{2,1,0:T(8,128)(2,1)S(1)}, bf16[3,16,512]{2,1,0:T(8,128)(2,1)S(1)}, u32[]{:S(2)}, u32[]{:S(2)}) collective-permute-start(bf16[3,16,512]{2,1,0:T(8,128)(2,1)S(1)} %get-tuple-element.191), channel_id=1, source_target_pairs={{0,2},{1,3},{4,6},{5,7},{8,10},{9,11},{12,14},{13,15},{16,18},{17,... | collective-permute-start | bytes 147464 | tf_op jit(solution)/shard_map/ppermute | solution.py:22
  74.0 10.1 %collective-permute-start.13 = (bf16[3,16,512]{2,1,0:T(8,128)(2,1)S(1)}, bf16[3,16,512]{2,1,0:T(8,128)(2,1)S(1)}, u32[]{:S(2)}, u32[]{:S(2)}) collective-permute-start(bf16[3,16,512]{2,1,0:T(8,128)(2,1)S(1)} %get-tuple-element.192), channel_id=1, source_target_pairs={{2,0},{3,1},{6,4},{7,5},{10,8},{11,9},{14,12},{15,13},{18,16},{19,... | collective-permute-start | bytes 147464 | tf_op jit(solution)/shard_map/ppermute | solution.py:24
  76.5 7.6 %collective-permute-start.11 = (bf16[6,16,512]{2,1,0:T(8,128)(2,1)S(1)}, bf16[6,16,512]{2,1,0:T(8,128)(2,1)S(1)}, u32[]{:S(2)}, u32[]{:S(2)}) collective-permute-start(bf16[6,16,512]{2,1,0:T(8,128)(2,1)S(1)} %pad_maximum_fusion.16), channel_id=1, source_target_pairs={{0,8},{1,9},{4,12},{5,13},{8,0},{9,1},{12,4},{13,5},{2,10},{3,11},... | collective-permute-start | bytes 294920 | tf_op jit(solution)/shard_map/ppermute | solution.py:34
  76.5 11.5 %copy-start.161 = (f32[2048]{0:T(1024)S(1)}, f32[2048]{0:T(1024)}, u32[]{:S(2)}) copy-start(f32[2048]{0:T(1024)} %get-tuple-element.518) | copy-start | bytes 24580
  78.3 9.9 %copy-start.139 = (f32[512]{0:T(512)S(1)}, f32[512]{0:T(512)}, u32[]{:S(2)}) copy-start(f32[512]{0:T(512)} %get-tuple-element.70) | copy-start | bytes 6148
  78.3 9.9 %copy-start.140 = (f32[512]{0:T(512)S(1)}, f32[512]{0:T(512)}, u32[]{:S(2)}) copy-start(f32[512]{0:T(512)} %get-tuple-element.71) | copy-start | bytes 6148
  84.2 8.0 %collective-permute-start.14 = (bf16[14,3,512]{2,1,0:T(4,128)(2,1)S(1)}, bf16[14,3,512]{2,1,0:T(4,128)(2,1)S(1)}, u32[]{:S(2)}, u32[]{:S(2)}) collective-permute-start(bf16[14,3,512]{2,1,0:T(4,128)(2,1)S(1)} %get-tuple-element.179), channel_id=1, source_target_pairs={{0,1},{1,4},{4,5},{5,8},{8,9},{9,12},{12,13},{13,0},{2,3},{3,6},{6... | collective-permute-start | bytes 129032 | tf_op jit(solution)/shard_map/ppermute | solution.py:22
  84.3 7.9 %collective-permute-start.15 = (bf16[14,3,512]{2,1,0:T(4,128)(2,1)S(1)}, bf16[14,3,512]{2,1,0:T(4,128)(2,1)S(1)}, u32[]{:S(2)}, u32[]{:S(2)}) collective-permute-start(bf16[14,3,512]{2,1,0:T(4,128)(2,1)S(1)} %get-tuple-element.180), channel_id=1, source_target_pairs={{1,0},{4,1},{5,4},{8,5},{9,8},{12,9},{13,12},{0,13},{3,2},{6,3},{7... | collective-permute-start | bytes 129032 | tf_op jit(solution)/shard_map/ppermute | solution.py:24
  105.3 1.4 collective-permute-start.24
  107.5 126.4 %reduce-scatter.18.cloned.1.call-start = ((), (), s32[]{:S(2)}) async-start(), calls=%async_computation.10 | async-start | bytes 2228224
  111.9 186.4 %reduce-scatter.14.cloned.1.call-start = ((), (), s32[]{:S(2)}) async-start(), calls=%async_computation.8 | async-start | bytes 2228224 | tf_op jit(solution)/shard_map/reduce_scatter | solution.py:206
  115.0 247.7 %reduce-scatter.12.cloned.1.call-start = ((), (), s32[]{:S(2)}) async-start(), calls=%async_computation.7 | async-start | bytes 2228224 | tf_op jit(solution)/shard_map/reduce_scatter | solution.py:206
  115.5 11.0 %copy-start.80 = (f32[1,1,512]{2,1,0:T(1,128)}, f32[1,1,512]{2,1,0:T(1,128)S(1)}, u32[]{:S(2)}) copy-start(f32[1,1,512]{2,1,0:T(1,128)S(1)} %get-tuple-element.214) | copy-start | bytes 6148
  115.5 11.0 %copy-start.82 = (f32[1,1,512]{2,1,0:T(1,128)}, f32[1,1,512]{2,1,0:T(1,128)S(1)}, u32[]{:S(2)}) copy-start(f32[1,1,512]{2,1,0:T(1,128)S(1)} %get-tuple-element.218) | copy-start | bytes 6148
  115.5 11.0 %copy-start.84 = (f32[1,1,512]{2,1,0:T(1,128)}, f32[1,1,512]{2,1,0:T(1,128)S(1)}, u32[]{:S(2)}) copy-start(f32[1,1,512]{2,1,0:T(1,128)S(1)} %get-tuple-element.219) | copy-start | bytes 6148
  115.5 11.0 %copy-start.86 = (f32[1,1,512]{2,1,0:T(1,128)}, f32[1,1,512]{2,1,0:T(1,128)S(1)}, u32[]{:S(2)}) copy-start(f32[1,1,512]{2,1,0:T(1,128)S(1)} %get-tuple-element.220) | copy-start | bytes 6148
  115.5 11.0 %copy-start.88 = (f32[1,1,512]{2,1,0:T(1,128)}, f32[1,1,512]{2,1,0:T(1,128)S(1)}, u32[]{:S(2)}) copy-start(f32[1,1,512]{2,1,0:T(1,128)S(1)} %get-tuple-element.221) | copy-start | bytes 6148
  115.5 11.0 %copy-start.90 = (f32[1,1,512]{2,1,0:T(1,128)}, f32[1,1,512]{2,1,0:T(1,128)S(1)}, u32[]{:S(2)}) copy-start(f32[1,1,512]{2,1,0:T(1,128)S(1)} %get-tuple-element.222) | copy-start | bytes 6148
  115.5 11.0 %copy-start.92 = (f32[1,1,512]{2,1,0:T(1,128)}, f32[1,1,512]{2,1,0:T(1,128)S(1)}, u32[]{:S(2)}) copy-start(f32[1,1,512]{2,1,0:T(1,128)S(1)} %get-tuple-element.223) | copy-start | bytes 6148
  115.5 11.0 %copy-start.94 = (f32[1,1,512]{2,1,0:T(1,128)}, f32[1,1,512]{2,1,0:T(1,128)S(1)}, u32[]{:S(2)}) copy-start(f32[1,1,512]{2,1,0:T(1,128)S(1)} %get-tuple-element.224) | copy-start | bytes 6148
  115.6 11.0 %copy-start.96 = (f32[1,1,512]{2,1,0:T(1,128)}, f32[1,1,512]{2,1,0:T(1,128)S(1)}, u32[]{:S(2)}) copy-start(f32[1,1,512]{2,1,0:T(1,128)S(1)} %get-tuple-element.225) | copy-start | bytes 6148
  115.6 11.0 %copy-start.98 = (f32[1,1,512]{2,1,0:T(1,128)}, f32[1,1,512]{2,1,0:T(1,128)S(1)}, u32[]{:S(2)}) copy-start(f32[1,1,512]{2,1,0:T(1,128)S(1)} %get-tuple-element.226) | copy-start | bytes 6148
  115.6 11.0 %copy-start.100 = (f32[1,1,512]{2,1,0:T(1,128)}, f32[1,1,512]{2,1,0:T(1,128)S(1)}, u32[]{:S(2)}) copy-start(f32[1,1,512]{2,1,0:T(1,128)S(1)} %get-tuple-element.227) | copy-start | bytes 6148
  115.6 11.0 %copy-start.102 = (f32[1,1,512]{2,1,0:T(1,128)}, f32[1,1,512]{2,1,0:T(1,128)S(1)}, u32[]{:S(2)}) copy-start(f32[1,1,512]{2,1,0:T(1,128)S(1)} %get-tuple-element.228) | copy-start | bytes 6148
  115.6 11.0 %copy-start.104 = (f32[1,1,512]{2,1,0:T(1,128)}, f32[1,1,512]{2,1,0:T(1,128)S(1)}, u32[]{:S(2)}) copy-start(f32[1,1,512]{2,1,0:T(1,128)S(1)} %get-tuple-element.229) | copy-start | bytes 6148
  115.6 11.0 %copy-start.106 = (f32[1,1,512]{2,1,0:T(1,128)}, f32[1,1,512]{2,1,0:T(1,128)S(1)}, u32[]{:S(2)}) copy-start(f32[1,1,512]{2,1,0:T(1,128)S(1)} %get-tuple-element.230) | copy-start | bytes 6148
  115.6 11.0 %copy-start.108 = (f32[1,1,512]{2,1,0:T(1,128)}, f32[1,1,512]{2,1,0:T(1,128)S(1)}, u32[]{:S(2)}) copy-start(f32[1,1,512]{2,1,0:T(1,128)S(1)} %get-tuple-element.231) | copy-start | bytes 6148
  115.6 11.0 %copy-start.110 = (f32[1,1,512]{2,1,0:T(1,128)}, f32[1,1,512]{2,1,0:T(1,128)S(1)}, u32[]{:S(2)}) copy-start(f32[1,1,512]{2,1,0:T(1,128)S(1)} %get-tuple-element.232) | copy-start | bytes 6148
  116.3 10.4 %copy-start.112 = (f32[1,1,512]{2,1,0:T(1,128)}, f32[1,1,512]{2,1,0:T(1,128)S(1)}, u32[]{:S(2)}) copy-start(f32[1,1,512]{2,1,0:T(1,128)S(1)} %get-tuple-element.195) | copy-start | bytes 6148
  120.8 306.4 %reduce-scatter.16.cloned.1.call-start = ((), (), s32[]{:S(2)}) async-start(), calls=%async_computation.9 | async-start | bytes 2228224
  128.0 15.9 %collective-permute-start.10 = (bf16[8,16,512]{2,1,0:T(8,128)(2,1)}, bf16[8,16,512]{2,1,0:T(8,128)(2,1)S(1)}, u32[]{:S(2)}, u32[]{:S(2)}) collective-permute-start(bf16[8,16,512]{2,1,0:T(8,128)(2,1)} %get-tuple-element.164), channel_id=1, source_target_pairs={{0,1},{1,0},{2,3},{3,2},{4,5},{5,4},{6,7},{7,6},{8,9},{9,8},{10,11... | collective-permute-start | bytes 393224 | tf_op jit(solution)/shard_map/ppermute | solution.py:38
  128.9 9.0 %collective-permute-start.16 = (bf16[6,16,512]{2,1,0:T(8,128)(2,1)}, bf16[6,16,512]{2,1,0:T(8,128)(2,1)}, u32[]{:S(2)}, u32[]{:S(2)}) collective-permute-start(bf16[6,16,512]{2,1,0:T(8,128)(2,1)} %pad_maximum_fusion.17), channel_id=1, source_target_pairs={{0,8},{1,9},{4,12},{5,13},{8,0},{9,1},{12,4},{13,5},{2,10},{3,11},... | collective-permute-start | bytes 294920 | tf_op jit(solution)/shard_map/ppermute | solution.py:34
  129.7 9.0 %collective-permute-start.17 = (bf16[3,16,512]{2,1,0:T(8,128)(2,1)S(1)}, bf16[3,16,512]{2,1,0:T(8,128)(2,1)S(1)}, u32[]{:S(2)}, u32[]{:S(2)}) collective-permute-start(bf16[3,16,512]{2,1,0:T(8,128)(2,1)S(1)} %get-tuple-element.189), channel_id=1, source_target_pairs={{0,2},{1,3},{4,6},{5,7},{8,10},{9,11},{12,14},{13,15},{16,18},{17,... | collective-permute-start | bytes 147464 | tf_op jit(solution)/shard_map/ppermute | solution.py:22
  134.0 6.0 %collective-permute-start.18 = (bf16[3,16,512]{2,1,0:T(8,128)(2,1)S(1)}, bf16[3,16,512]{2,1,0:T(8,128)(2,1)S(1)}, u32[]{:S(2)}, u32[]{:S(2)}) collective-permute-start(bf16[3,16,512]{2,1,0:T(8,128)(2,1)S(1)} %get-tuple-element.190), channel_id=1, source_target_pairs={{2,0},{3,1},{6,4},{7,5},{10,8},{11,9},{14,12},{15,13},{18,16},{19,... | collective-permute-start | bytes 147464 | tf_op jit(solution)/shard_map/ppermute | solution.py:24
  140.1 6.1 %collective-permute-start.19 = (bf16[14,3,512]{2,1,0:T(4,128)(2,1)S(1)}, bf16[14,3,512]{2,1,0:T(4,128)(2,1)S(1)}, u32[]{:S(2)}, u32[]{:S(2)}) collective-permute-start(bf16[14,3,512]{2,1,0:T(4,128)(2,1)S(1)} %get-tuple-element.175), channel_id=1, source_target_pairs={{0,1},{1,4},{4,5},{5,8},{8,9},{9,12},{12,13},{13,0},{2,3},{3,6},{6... | collective-permute-start | bytes 129032 | tf_op jit(solution)/shard_map/ppermute | solution.py:22
  140.3 5.9 %collective-permute-start.20 = (bf16[14,3,512]{2,1,0:T(4,128)(2,1)S(1)}, bf16[14,3,512]{2,1,0:T(4,128)(2,1)S(1)}, u32[]{:S(2)}, u32[]{:S(2)}) collective-permute-start(bf16[14,3,512]{2,1,0:T(4,128)(2,1)S(1)} %get-tuple-element.176), channel_id=1, source_target_pairs={{1,0},{4,1},{5,4},{8,5},{9,8},{12,9},{13,12},{0,13},{3,2},{6,3},{7... | collective-permute-start | bytes 129032 | tf_op jit(solution)/shard_map/ppermute | solution.py:24
  153.3 275.1 %collective-permute-start.21 = (bf16[8,16,512]{2,1,0:T(8,128)(2,1)S(1)}, bf16[8,16,512]{2,1,0:T(8,128)(2,1)S(1)}, u32[]{:S(2)}, u32[]{:S(2)}) collective-permute-start(bf16[8,16,512]{2,1,0:T(8,128)(2,1)S(1)} %broadcast_select_fusion.2), channel_id=1, source_target_pairs={{0,1},{1,0},{2,3},{3,2},{4,5},{5,4},{6,7},{7,6},{8,9},{9,8},{10,11... | collective-permute-start | bytes 393224 | tf_op jit(solution)/shard_map/ppermute | solution.py:38
  363.7 65.4 %collective-permute-start.23 = (bf16[128,512]{1,0:T(8,128)(2,1)S(1)}, bf16[128,512]{1,0:T(8,128)(2,1)S(1)}, u32[]{:S(2)}, u32[]{:S(2)}) collective-permute-start(bf16[128,512]{1,0:T(8,128)(2,1)S(1)} %get-tuple-element.168), channel_id=1, source_target_pairs={{0,1},{1,0},{2,3},{3,2},{4,5},{5,4},{6,7},{7,6},{8,9},{9,8},{10,11... | collective-permute-start | bytes 393224 | tf_op jit(solution)/shard_map/ppermute | solution.py:38
  428.3 1.7 collective-permute-start.22
  (142 other events, 679.6 us)
Sparse Core Ops, SparseCore 0:
  9.5 16.4 all-gather.4
  27.6 14.7 all-gather.6
  107.6 61.7 reduce-scatter.19
  173.0 60.8 reduce-scatter.17
  237.5 60.7 reduce-scatter.13
  301.9 60.7 reduce-scatter.11
  366.4 60.7 reduce-scatter.15
where the time goes:
time: 439 us; the launch traced here: 438 us
  waiting for transfers between devices  287 us (65%)
  other arithmetic  45.5 us (10%)
  starting transfers between devices  38.2 us (9%)
  local copies, waits for them, and re-layouts  26.8 us (6%)
  matrix products  19.3 us (4%)
  between operations  17.5 us (4%)
    unnamed x10, waiting for transfers between devices  142 us
    reduce_scatter x2, waiting for transfers between devices, scattered(): lax.psum_scatter(value.astype(jnp.bfloat16), ('lon', 'lat', 'segment'), s...  128 us
    ppermute x8, starting transfers between devices, extended(): lax.ppermute(head, axis, [((i + 1) % count, i) for i in range(ends)])  19.1 us
    unnamed x360, local copies, waits for them, and re-layouts  15.3 us
    ppermute x8, starting transfers between devices, extended(): lax.ppermute(tail, axis, [(i, (i + 1) % count) for i in range(ends)])  13.9 us
    another operation x22, other arithmetic, correlate(): window * stencil[row_tap, col_tap].astype(jnp.float32)  13 us
    ppermute x4, waiting for transfers between devices, from_behind(): return lax.ppermute(value, axis, pairs)  8.82 us
  transfers between devices with their start and end apart: 32, of which 13 were waited for; matrix products, arithmetic and copies ran while one was open for 15% of the time, Pallas kernels for 0%

commit v1 on v0

--- a/solution.py
+++ b/solution.py
@@ -1,6 +1,9 @@
+import functools
 import jax
 import jax.numpy as jnp
 from jax import lax
+from jax.experimental import pallas as pl
+from jax.experimental.pallas import tpu as pltpu
 from jax.sharding import PartitionSpec as P
 
 KERNEL = 7
@@ -125,7 +128,7 @@
     down_sum = jnp.dot(hidden.T, scaled, preferred_element_type=jnp.float32)
     hidden_grad = jnp.dot(scaled, down_matrix.T, preferred_element_type=jnp.float32)
     before_grad = (hidden_grad * slope_value).astype(jnp.bfloat16)
-    up_sum = jnp.dot(normed.T, before_grad, preferred_element_type=jnp.float32)
+    up_sum = jnp.dot(before_grad.T, normed, preferred_element_type=jnp.float32)
     bias_sum = jnp.sum(before_grad.astype(jnp.float32), axis=0)
     normed_grad = jnp.dot(before_grad, up_matrix.T, preferred_element_type=jnp.float32).reshape(
         out_rows, out_cols, channels
@@ -202,10 +205,195 @@
     )
 
 
-def scattered(value, dim):
-    return lax.psum_scatter(
-        value.astype(jnp.bfloat16), ("lon", "lat", "segment"), scatter_dimension=dim, tiled=True
-    )
+def plan(lon, lat):
+    lon_bits, lat_bits = lon.bit_length() - 1, lat.bit_length() - 1
+    along_lon = [("lon", bit, lon_bits - 1 - bit) for bit in range(lon_bits)]
+    along_lat = [("lat", bit, lon_bits + lat_bits - 1 - bit) for bit in range(lat_bits)]
+    first = along_lat + along_lon
+    second = along_lon[:1] + along_lat + along_lon[1:]
+    return first, second
+
+
+def picked(axis, bit):
+    return (slice(None),) * axis + (bit,)
+
+
+def add_block(total, term, lead):
+    rows = total.shape[-2]
+    step = min(rows, 64)
+    per = rows // step
+    count = per
+    for size in lead:
+        count = count * size
+
+    def body(at, carry):
+        row = pl.multiple_of((at % per) * step, step)
+        rest = at // per
+        index = []
+        for size in reversed(lead):
+            index.insert(0, rest % size)
+            rest = rest // size
+        term(tuple(index), pl.ds(row, step))
+        return carry
+
+    lax.fori_loop(0, count, body, 0)
+
+
+def reduce_kernel(orders, depth, *refs):
+    parts = len(orders)
+    first, second = refs[:parts], refs[parts : 2 * parts]
+    outs = refs[2 * parts : 3 * parts]
+    slots = [refs[3 * parts + p * (depth + 1) : 3 * parts + (p + 1) * (depth + 1)] for p in range(parts)]
+    send_sem, recv_sem = refs[3 * parts + parts * (depth + 1) :]
+    core = lax.axis_index("segment")
+    place = {"lon": lax.axis_index("lon"), "lat": lax.axis_index("lat")}
+
+    def bit_of(step):
+        return (place[step[0]] // (1 << step[1])) % 2
+
+    def across(step):
+        own = bit_of(step)
+        return {step[0]: place[step[0]] + (1 - 2 * own) * (1 << step[1])}
+
+    barrier = pltpu.get_barrier_semaphore()
+    pl.semaphore_signal(
+        barrier, inc=1, device_id={"segment": 1 - core}, device_id_type=pl.DeviceIdType.MESH
+    )
+    for step in orders[0]:
+        pl.semaphore_signal(
+            barrier, inc=1, device_id=across(step), device_id_type=pl.DeviceIdType.MESH
+        )
+    pl.semaphore_wait(barrier, depth + 1)
+
+    def chip_copy(part, half, source):
+        step = orders[part][0]
+        bit = bit_of(step)
+        index = picked(step[2], 1 - bit if half == 0 else bit)
+        return pltpu.make_async_remote_copy(
+            src_ref=source.at[index],
+            dst_ref=slots[part][0].at[index],
+            send_sem=send_sem.at[part, half],
+            recv_sem=recv_sem.at[part, half],
+            device_id={"segment": 1 - core},
+            device_id_type=pl.DeviceIdType.MESH,
+        )
+
+    def axis_copy(part, stage):
+        step = orders[part][stage]
+        position = step[2] - sum(1 for done in orders[part][:stage] if done[2] < step[2])
+        return pltpu.make_async_remote_copy(
+            src_ref=slots[part][stage].at[picked(position, 1 - bit_of(step))],
+            dst_ref=slots[part][stage + 1],
+            send_sem=send_sem.at[part, 2 + stage],
+            recv_sem=recv_sem.at[part, 2 + stage],
+            device_id=across(step),
+            device_id_type=pl.DeviceIdType.MESH,
+        )
+
+    def position_of(part, stage):
+        step = orders[part][stage]
+        return step[2] - sum(1 for done in orders[part][:stage] if done[2] < step[2])
+
+    def add_into(target, source, fixed_at, bit, source_at, source_bit):
+        lead = target.shape[:-2]
+        if fixed_at is not None:
+            lead = lead[:fixed_at] + lead[fixed_at + 1 :]
+
+        def term(index, rows):
+            full = index
+            if fixed_at is not None:
+                full = index[:fixed_at] + (bit,) + index[fixed_at:]
+            taken = full
+            if source_at is not None:
+                taken = full[:source_at] + (source_bit,) + full[source_at:]
+            spot = full + (rows, slice(None))
+            total = target[spot].astype(jnp.float32) + source[
+                taken + (rows, slice(None))
+            ].astype(jnp.float32)
+            target[spot] = total.astype(target.dtype)
+
+        add_block(target, term, lead)
+
+    for half in range(2):
+        for part in range(parts):
+
+            @pl.when(core == 0)
+            def _():
+                chip_copy(part, half, second[part]).start()
+
+            @pl.when(core == 1)
+            def _():
+                chip_copy(part, half, first[part]).start()
+
+    for half in range(2):
+        for part in range(parts):
+            step = orders[part][0]
+            bit = bit_of(step)
+            bit = 1 - bit if half == 0 else bit
+            chip_copy(part, half, first[part]).wait_recv()
+
+            @pl.when(core == 0)
+            def _():
+                add_into(slots[part][0], first[part], step[2], bit, None, None)
+
+            @pl.when(core == 1)
+            def _():
+                add_into(slots[part][0], second[part], step[2], bit, None, None)
+
+            if half == 0:
+                axis_copy(part, 0).start()
+
+    for stage in range(depth):
+        for part in range(parts):
+            step = orders[part][stage]
+            source_at, own = position_of(part, stage), bit_of(step)
+            axis_copy(part, stage).wait_recv()
+            source, target = slots[part][stage], slots[part][stage + 1]
+            if stage + 1 < depth:
+                fixed_at, bit = position_of(part, stage + 1), bit_of(orders[part][stage + 1])
+                add_into(target, source, fixed_at, 1 - bit, source_at, own)
+                axis_copy(part, stage + 1).start()
+                add_into(target, source, fixed_at, bit, source_at, own)
+            else:
+                outs[part][...] = target[...].astype(jnp.float32) + source[
+                    picked(source_at, own)
+                ].astype(jnp.float32)
+    for part in range(parts):
+        for half in range(2):
+            chip_copy(part, half, first[part]).wait_send()
+        for stage in range(depth):
+            axis_copy(part, stage).wait_send()
+
+
+def reduced(first, second):
+    lon, lat = lax.axis_size("lon"), lax.axis_size("lat")
+    order_a, order_b = plan(lon, lat)
+    orders = (order_a, order_b, order_a)
+    depth = len(order_a)
+    lead = (2,) * depth
+    first = [value.astype(jnp.bfloat16).reshape(lead + value.shape[1:]) for value in first]
+    second = [value.astype(jnp.bfloat16).reshape(lead + value.shape[1:]) for value in second]
+    blocks = [value.shape[depth:] for value in first]
+    scratch = [
+        pltpu.VMEM((2,) * (depth - stage) + block, jnp.bfloat16)
+        for block in blocks
+        for stage in range(depth + 1)
+    ]
+    vmem = pl.BlockSpec(memory_space=pltpu.VMEM)
+    return pl.pallas_call(
+        functools.partial(reduce_kernel, orders, depth),
+        out_shape=[jax.ShapeDtypeStruct(block, jnp.float32) for block in blocks],
+        in_specs=[vmem] * (2 * len(blocks)),
+        out_specs=[vmem] * len(blocks),
+        scratch_shapes=scratch
+        + [
+            pltpu.SemaphoreType.DMA((len(blocks), depth + 2)),
+            pltpu.SemaphoreType.DMA((len(blocks), depth + 2)),
+        ],
+        compiler_params=pltpu.CompilerParams(
+            collective_id=0, has_side_effects=True, vmem_limit_bytes=48 * 1024 * 1024
+        ),
+    )(*first, *second)
 
 
 def packed(sums):
@@ -215,7 +403,19 @@
     bias_rows = (
         bias_sum.reshape(pieces, -1, channels // pieces).transpose(1, 0, 2).reshape(-1, channels)
     )
-    return jnp.concatenate([stencil_sum, vectors, bias_rows], axis=0)
+    rows = jnp.concatenate([stencil_sum, vectors, bias_rows], axis=0)
+    rows = rows.reshape(rows.shape[0], pieces, channels // pieces).transpose(1, 0, 2)
+    return jnp.pad(rows, ((0, 0), (0, -rows.shape[1] % 16), (0, -rows.shape[2] % 128)))
+
+
+def chunked(sums):
+    pieces = lax.axis_size(("lon", "lat"))
+    up_sum, down_sum = sums[:2]
+    return (
+        up_sum.reshape(pieces, -1, up_sum.shape[1]),
+        down_sum.reshape(pieces, -1, down_sum.shape[1]),
+        packed(sums),
+    )
 
 
 def local(
@@ -272,29 +472,19 @@
     second_grad, second_sums = backward_section(
         second_stored, cotangent, sections[1], extender, north_weight, south_weight
     )
-    up_second = scattered(second_sums[0], 1)
-    down_second = scattered(second_sums[1], 0)
     first_grad, first_sums = backward_section(
         first_stored, second_grad, sections[0], extender, north_weight, south_weight
     )
-    up_first = scattered(first_sums[0], 1)
-    down_first = scattered(first_sums[1], 0)
     section_out = both_halves(leading, first_out, second_out, 1)[None]
     boundary_grad = both_halves(leading, first_grad, second_grad, 1)[None]
-    up_part = both_halves(leading, up_first, up_second, 1).astype(jnp.float32)
-    down_part = both_halves(leading, down_first, down_second, 0).astype(jnp.float32)
-    first_small = packed(first_sums)
-    second_small = packed(second_sums)
-    small = jnp.where(leading, first_small, second_small) + hand_over(
-        jnp.where(leading, second_small, first_small)
-    )
-    small = lax.psum_scatter(
-        small.astype(jnp.bfloat16), ("lon", "lat"), scatter_dimension=1, tiled=True
-    ).astype(jnp.float32)
+    up_part, down_part, small = reduced(chunked(first_sums), chunked(second_sums))
+    up_part = up_part.T
+    small = small[:, : channels // lax.axis_size(("lon", "lat"))]
     count = KERNEL * KERNEL
     stencil_part = small[:count]
     vector_part = small[count : count + 5]
-    bias_part = small[count + 5 :].reshape(-1)
+    bias_count = hidden_bias.shape[1] // channels
+    bias_part = small[count + 5 : count + 5 + bias_count].reshape(-1)
     return (
         section_out,
         boundary_grad,

time: 439 us -> 252 us (0.57)
  waiting for transfers between devices: 287 us -> 7.61 us
  Pallas kernels: 0 us -> 70.9 us
  starting transfers between devices: 38.2 us -> 45.7 us
  other arithmetic: 45.5 us -> 51.7 us
  local copies, waits for them, and re-layouts: 26.8 us -> 31.3 us
    unnamed x10 -> x2, waiting for transfers between devices: 142 us -> 0.7 us
    reduce_scatter x2 -> x0, waiting for transfers between devices: 128 us -> none  [scattered(): lax.psum_scatter(value.astype(jnp.bfloat16), ('lon', 'lat', 'segment'), s...]
    pallas_call x0 -> x1, Pallas kernels: none -> 70.9 us  [reduced(): pl.pallas_call(functools.partial(reduce_kernel, orders, depth), out_shape...]
    unnamed x360 -> x384, local copies, waits for them, and re-layouts: 15.3 us -> 6.9 us
    ppermute x4, waiting for transfers between devices: 8.82 us -> 1.17 us  [from_behind(): return lax.ppermute(value, axis, pairs)]
    ppermute x8, starting transfers between devices: 13.9 us -> 21.5 us  [extended(): lax.ppermute(tail, axis, [(i, (i + 1) % count) for i in range(ends)])]
    concatenate x2 -> x110, local copies, waits for them, and re-layouts: 4.07 us -> 10.2 us  [packed(): rows = jnp.concatenate([stencil_sum, vectors, bias_rows], axis=0)]
    dot_general x0 -> x4, local copies, waits for them, and re-layouts: none -> 5.04 us  [the longest x2 3.04 us: backward_section(): up_sum = jnp.dot(before_grad.T, normed, preferred_element_type=jnp.float32)]
  transfers between devices with their start and end apart: 32 -> 24, of which waited for: 13 -> 7; matrix products, arithmetic and copies ran while one was open for 15% -> 29% of each run, Pallas kernels for 0% -> 28%
where the time goes in v1:
time: 252 us; the launch traced here: 251 us
  Pallas kernels  70.9 us (28%)
  other arithmetic  51.7 us (21%)
  starting transfers between devices  45.7 us (18%)
  local copies, waits for them, and re-layouts  31.3 us (12%)
  matrix products  22.2 us (9%)
  between operations  17.2 us (7%)
  waiting for transfers between devices  7.61 us (3%)
  blocking collectives  3.79 us (2%)
    pallas_call x1, Pallas kernels, reduced(): pl.pallas_call(functools.partial(reduce_kernel, orders, depth), out_shape...  70.9 us
    ppermute x8, starting transfers between devices, extended(): lax.ppermute(tail, axis, [(i, (i + 1) % count) for i in range(ends)])  21.5 us
    ppermute x8, starting transfers between devices, extended(): lax.ppermute(head, axis, [((i + 1) % count, i) for i in range(ends)])  19 us
    another operation x22, other arithmetic, correlate(): window * stencil[row_tap, col_tap].astype(jnp.float32)  14.9 us
    concatenate x110, local copies, waits for them, and re-layouts, packed(): rows = jnp.concatenate([stencil_sum, vectors, bias_rows], axis=0)  10.2 us
    unnamed x384, local copies, waits for them, and re-layouts  6.9 us
    slice x10, local copies, waits for them, and re-layouts, correlate(): stencil[row_tap, col_tap].astype(jnp.float32)  6.5 us
    reduce_sum x8, other arithmetic, stencil_terms(): columns.append(jnp.sum(window * grad_wide, axis=(0, 1)))  5.85 us
  transfers between devices with their start and end apart: 24, of which 7 were waited for; matrix products, arithmetic and copies ran while one was open for 29% of the time, Pallas kernels for 28%

profile of v1, /device:TPU:0, one launch (start us, length us, event | category | flops | bytes accessed | tf_op | source)
XLA Modules:
  0.0 250.5 jit_solution(15226707055463912360)
XLA Ops:
  8.1 1.3 collective-permute-start.2
  9.4 4.9 %collective-permute-start.1 = (bf16[3,16,512]{2,1,0:T(8,128)(2,1)S(1)}, bf16[3,16,512]{2,1,0:T(8,128)(2,1)S(1)}, u32[]{:S(2)}, u32[]{:S(2)}) collective-permute-start(bf16[3,16,512]{2,1,0:T(8,128)(2,1)S(1)} %get-tuple-element.186), channel_id=1, source_target_pairs={{0,2},{1,3},{4,6},{5,7},{8,10},{9,11},{12,14},{13,15},{16,18},{17,... | collective-permute-start | bytes 147464 | tf_op jit(solution)/shard_map/ppermute | solution.py:25
  14.3 3.8 %collective-permute-start = (bf16[6,16,512]{2,1,0:T(8,128)(2,1)S(1)}, bf16[6,16,512]{2,1,0:T(8,128)(2,1)S(1)}, u32[]{:S(2)}, u32[]{:S(2)}) collective-permute-start(bf16[6,16,512]{2,1,0:T(8,128)(2,1)S(1)} %pad_maximum_fusion.14), channel_id=1, source_target_pairs={{0,8},{1,9},{4,12},{5,13},{8,0},{9,1},{12,4},{13,5},{2,10},{3,11},... | collective-permute-start | bytes 294920 | tf_op jit(solution)/shard_map/ppermute | solution.py:37
  18.2 1.9 all_gather.17
  21.6 1.9 all-gather.1
  34.7 1.3 broadcast_multiply_fusion.41
  36.0 1.3 broadcast_multiply_fusion.43
  37.3 1.3 broadcast_multiply_fusion.45
  45.8 1.4 fusion.343
  47.2 1.4 fusion.337
  49.2 3.4 %collective-permute-start.4 = (bf16[14,3,512]{2,1,0:T(4,128)(2,1)S(1)}, bf16[14,3,512]{2,1,0:T(4,128)(2,1)S(1)}, u32[]{:S(2)}, u32[]{:S(2)}) collective-permute-start(bf16[14,3,512]{2,1,0:T(4,128)(2,1)S(1)} %get-tuple-element.203), channel_id=1, source_target_pairs={{1,0},{4,1},{5,4},{8,5},{9,8},{12,9},{13,12},{0,13},{3,2},{6,3},{7... | collective-permute-start | bytes 129032 | tf_op jit(solution)/shard_map/ppermute | solution.py:27
  53.2 1.8 collective-permute-done.3
  55.1 2.6 %fusion.354 = (f32[8,16]{1,0:T(8,128)S(1)}, f32[8,16,512]{2,1,0:T(8,128)S(1)}) fusion(f32[512]{0:T(512)S(1)} %bitcast.762, f32[512]{0:T(512)S(1)} %bitcast.713, bf16[14,19,512]{2,1,0:T(8,128)(2,1)S(1)} %get-tuple-element.201, f32[512]{0:T(512)S(1)} %bitcast.714, f32[512]{0:T(512)S(1)} %bitcast.715, f32[512]{0:T(512)S(1)} %bitcast.716, ...), kind=kLoop, calls=%fused_computation.849 | loop fusion | flops 10092416 | bytes 6099456 | tf_op jit(solution)/shard_map/reduce_sum | solution.py:88
  58.3 2.1 convolution_add_fusion.1
  60.4 2.4 fusion.15
  63.7 1.3 collective-permute-start.7
  65.0 4.5 %collective-permute-start.6 = (bf16[3,16,512]{2,1,0:T(8,128)(2,1)S(1)}, bf16[3,16,512]{2,1,0:T(8,128)(2,1)S(1)}, u32[]{:S(2)}, u32[]{:S(2)}) collective-permute-start(bf16[3,16,512]{2,1,0:T(8,128)(2,1)S(1)} %get-tuple-element.208), channel_id=1, source_target_pairs={{0,2},{1,3},{4,6},{5,7},{8,10},{9,11},{12,14},{13,15},{16,18},{17,... | collective-permute-start | bytes 147464 | tf_op jit(solution)/shard_map/ppermute | solution.py:25
  69.5 1.2 collective-permute-done.5
  71.4 3.5 %collective-permute-start.9 = (bf16[14,3,512]{2,1,0:T(4,128)(2,1)S(1)}, bf16[14,3,512]{2,1,0:T(4,128)(2,1)S(1)}, u32[]{:S(2)}, u32[]{:S(2)}) collective-permute-start(bf16[14,3,512]{2,1,0:T(4,128)(2,1)S(1)} %get-tuple-element.199), channel_id=1, source_target_pairs={{1,0},{4,1},{5,4},{8,5},{9,8},{12,9},{13,12},{0,13},{3,2},{6,3},{7... | collective-permute-start | bytes 129032 | tf_op jit(solution)/shard_map/ppermute | solution.py:27
  75.5 1.5 collective-permute-done.8
  77.1 2.6 %fusion.352 = (f32[8,16]{1,0:T(8,128)S(1)}, f32[8,16,512]{2,1,0:T(8,128)S(1)}) fusion(f32[512]{0:T(512)S(1)} %bitcast.662, f32[512]{0:T(512)S(1)} %bitcast.664, bf16[14,19,512]{2,1,0:T(8,128)(2,1)S(1)} %get-tuple-element.197, f32[512]{0:T(512)S(1)} %bitcast.665, f32[512]{0:T(512)S(1)} %bitcast.666, f32[512]{0:T(512)S(1)} %bitcast.667, ...), kind=kLoop, calls=%fused_computation.848 | loop fusion | flops 10092416 | bytes 6099456 | tf_op jit(solution)/shard_map/reduce_sum | solution.py:88
  80.9 1.1 fusion.304
  82.0 0.8 fusion.346
  82.8 1.6 fusion.344
  84.5 1.5 multiply_reduce_fusion
  86.1 1.3 collective-permute-start.13
  87.5 5.8 %collective-permute-start.12 = (bf16[3,16,512]{2,1,0:T(8,128)(2,1)S(1)}, bf16[3,16,512]{2,1,0:T(8,128)(2,1)}, u32[]{:S(2)}, u32[]{:S(2)}) collective-permute-start(bf16[3,16,512]{2,1,0:T(8,128)(2,1)S(1)} %get-tuple-element.206), channel_id=1, source_target_pairs={{0,2},{1,3},{4,6},{5,7},{8,10},{9,11},{12,14},{13,15},{16,18},{17,... | collective-permute-start | bytes 147464 | tf_op jit(solution)/shard_map/ppermute | solution.py:25
  93.2 0.9 fusion.228
  94.1 1.1 fusion.229
  95.8 1.0 collective-permute-start.11
  96.8 1.3 fusion.43
  98.0 2.0 copy.257
  100.1 1.0 copy.258
  101.1 3.2 %convolution_convert_fusion.1 = bf16[8,256,512]{2,1,0:T(8,128)(2,1)} fusion(bf16[8,256,128]{2,1,0:T(8,128)(2,1)} %bitcast.456, bf16[128,512,1]{1,0,2:T(8,128)(2,1)S(1)} %bitcast.463), kind=kOutput, calls=%fused_computation.111 | convolution fusion | flops 269484032 | bytes 2752512 | tf_op jit(solution)/shard_map/dot_general | solution.py:131
  104.4 2.0 convolution_convert_fusion
  111.9 0.8 reverse_select_fusion.2
  113.1 3.4 %collective-permute-start.15 = (bf16[14,3,512]{2,1,0:T(4,128)(2,1)S(1)}, bf16[14,3,512]{2,1,0:T(4,128)(2,1)S(1)}, u32[]{:S(2)}, u32[]{:S(2)}) collective-permute-start(bf16[14,3,512]{2,1,0:T(4,128)(2,1)S(1)} %get-tuple-element.195), channel_id=1, source_target_pairs={{1,0},{4,1},{5,4},{8,5},{9,8},{12,9},{13,12},{0,13},{3,2},{6,3},{7... | collective-permute-start | bytes 129032 | tf_op jit(solution)/shard_map/ppermute | solution.py:27
  116.5 0.8 maximum_select_fusion
  117.2 1.1 collective-permute-done.14
  119.1 1.0 add_multiply_fusion.4
  120.1 1.4 add_multiply_fusion.5
  121.8 3.9 %fusion.305 = (bf16[512]{0:T(512)(128)(2,1)}, bf16[8,16,512]{2,1,0:T(8,128)(2,1)S(1)}) fusion(f32[128,512]{1,0:T(8,128)S(1)} %fusion.15, f32[3,16,512]{2,1,0:T(8,128)S(1)} %add_multiply_fusion.4, f32[3,16,512]{2,1,0:T(8,128)S(1)} %add_multiply_fusion.5, f32[512]{0:T(512)S(1)} %bitcast.621, bf16[14,19,512]{2,1,0:T(8,128)(2,1)S(1)} %get-tuple-element.193, ...), kind=kLoop, calls=%fused_computation.540 | loop fusion | flops 11271680 | bytes 6556676 | tf_op jit(solution)/shard_map/reduce_sum | solution.py:125
  125.8 1.6 fusion.348
  128.0 1.5 multiply_reduce_fusion.1
  129.6 1.3 collective-permute-start.18
  131.6 5.8 %collective-permute-start.17 = (bf16[3,16,512]{2,1,0:T(8,128)(2,1)S(1)}, bf16[3,16,512]{2,1,0:T(8,128)(2,1)}, u32[]{:S(2)}, u32[]{:S(2)}) collective-permute-start(bf16[3,16,512]{2,1,0:T(8,128)(2,1)S(1)} %get-tuple-element.204), channel_id=1, source_target_pairs={{0,2},{1,3},{4,6},{5,7},{8,10},{9,11},{12,14},{13,15},{16,18},{17,... | collective-permute-start | bytes 147464 | tf_op jit(solution)/shard_map/ppermute | solution.py:25
  137.3 0.8 fusion.302
  138.2 1.2 fusion.303
  139.3 1.1 fusion.299
  141.1 1.0 copy.255
  142.1 1.0 copy.256
  143.2 1.8 convolution_convert_fusion.3
  145.2 2.9 %convolution_convert_fusion.2 = bf16[8,256,512]{2,1,0:T(8,128)(2,1)} fusion(bf16[8,256,128]{2,1,0:T(8,128)(2,1)S(1)} %bitcast.459, bf16[128,512,1]{1,0,2:T(8,128)(2,1)} %bitcast.470), kind=kOutput, calls=%fused_computation.112 | convolution fusion | flops 269484032 | bytes 2752512 | tf_op jit(solution)/shard_map/dot_general | solution.py:128
  153.6 1.6 copy-done
  155.2 70.9 %shard_map.162 = (f32[256,512]{1,0:T(8,128)S(1)}, f32[256,512]{1,0:T(8,128)S(1)}, f32[64,128]{1,0:T(8,128)S(1)}) custom-call(bf16[2,2,2,256,512]{4,3,2,1,0:T(8,128)(2,1)S(1)} %bitcast.448, bf16[2,2,2,256,512]{4,3,2,1,0:T(8,128)(2,1)S(1)} %bitcast.449, bf16[2,2,2,64,128]{4,3,2,1,0:T(8,128)(2,1)S(1)} %bitcast.451, bf16[2,2,2,256,512]{4,3,2,1,0:T(8,128)(2,1)} %bitcast.454, ...), custom_call_target="tpu_custom_call" | custom-call | tf_op jit(solution)/shard_map/pallas_call | solution.py:383
  226.2 0.8 fusion.366
  227.0 0.8 reverse_select_fusion
  228.2 3.5 %collective-permute-start.20 = (bf16[14,3,512]{2,1,0:T(4,128)(2,1)S(1)}, bf16[14,3,512]{2,1,0:T(4,128)(2,1)S(1)}, u32[]{:S(2)}, u32[]{:S(2)}) collective-permute-start(bf16[14,3,512]{2,1,0:T(4,128)(2,1)S(1)} %get-tuple-element.191), channel_id=1, source_target_pairs={{1,0},{4,1},{5,4},{8,5},{9,8},{12,9},{13,12},{0,13},{3,2},{6,3},{7... | collective-permute-start | bytes 129032 | tf_op jit(solution)/shard_map/ppermute | solution.py:27
  231.8 1.0 copy.252
  235.0 0.9 add_multiply_fusion.2
  235.9 1.4 add_multiply_fusion.3
  237.5 3.2 %select_bitcast_fusion = (bf16[1,8,16,512]{3,2,1,0:T(8,128)(2,1)S(1)}, bf16[8,16,512]{2,1,0:T(8,128)(2,1)S(1)}) fusion(bf16[8,16,512]{2,1,0:T(8,128)(2,1)S(1)} %copy-done.6, pred[]{:T(512)S(6)} %eq.9, f32[3,16,512]{2,1,0:T(8,128)S(1)} %add_multiply_fusion.2, f32[3,16,512]{2,1,0:T(8,128)S(1)} %add_multiply_fusion.3, f32[512]{0:T(512)S(1)} %bitcast.572, ...), kind=kLoop, calls=%fused_computation.627 | loop fusion | flops 10354688 | bytes 6424577 | tf_op jit(solution)/shard_map/concatenate | solution.py:203
  242.1 0.8 maximum_select_fusion.1
  242.9 0.8 copy.262
  (634 shorter events, 43.4 us)
Async XLA Ops:
  7.2 51.1 %all-gather.5.cloned.1.call-start = ((), (), s32[]{:S(2)}) async-start(), calls=%async_computation | async-start | bytes 6291456 | tf_op jit(solution)/shard_map/all_gather | solution.py:445
  7.9 13.5 %copy-start.174 = (f32[1,512]{1,0:T(1,128)S(1)}, f32[1,512]{1,0:T(1,128)}, u32[]{:S(2)}) copy-start(f32[1,512]{1,0:T(1,128)} %param.14) | copy-start | bytes 6148
  7.9 13.5 %copy-start.175 = (f32[1,512]{1,0:T(1,128)S(1)}, f32[1,512]{1,0:T(1,128)}, u32[]{:S(2)}) copy-start(f32[1,512]{1,0:T(1,128)} %param.15) | copy-start | bytes 6148
  8.0 13.5 %copy-start.176 = (f32[1,512]{1,0:T(1,128)S(1)}, f32[1,512]{1,0:T(1,128)}, u32[]{:S(2)}) copy-start(f32[1,512]{1,0:T(1,128)} %param.16) | copy-start | bytes 6148
  8.0 52.4 %all-gather.7.cloned.1.call-start = ((), (), s32[]{:S(2)}) async-start(), calls=%async_computation.1 | async-start | bytes 6291456 | tf_op jit(solution)/shard_map/all_gather | solution.py:445
  8.1 40.8 %collective-permute-start.2 = (bf16[3,16,512]{2,1,0:T(8,128)(2,1)S(1)}, bf16[3,16,512]{2,1,0:T(8,128)(2,1)S(1)}, u32[]{:S(2)}, u32[]{:S(2)}) collective-permute-start(bf16[3,16,512]{2,1,0:T(8,128)(2,1)S(1)} %get-tuple-element.187), channel_id=1, source_target_pairs={{2,0},{3,1},{6,4},{7,5},{10,8},{11,9},{14,12},{15,13},{18,16},{19,... | collective-permute-start | bytes 147464 | tf_op jit(solution)/shard_map/ppermute | solution.py:27
  9.4 39.5 %collective-permute-start.1 = (bf16[3,16,512]{2,1,0:T(8,128)(2,1)S(1)}, bf16[3,16,512]{2,1,0:T(8,128)(2,1)S(1)}, u32[]{:S(2)}, u32[]{:S(2)}) collective-permute-start(bf16[3,16,512]{2,1,0:T(8,128)(2,1)S(1)} %get-tuple-element.186), channel_id=1, source_target_pairs={{0,2},{1,3},{4,6},{5,7},{8,10},{9,11},{12,14},{13,15},{16,18},{17,... | collective-permute-start | bytes 147464 | tf_op jit(solution)/shard_map/ppermute | solution.py:25
  14.3 34.5 %collective-permute-start = (bf16[6,16,512]{2,1,0:T(8,128)(2,1)S(1)}, bf16[6,16,512]{2,1,0:T(8,128)(2,1)S(1)}, u32[]{:S(2)}, u32[]{:S(2)}) collective-permute-start(bf16[6,16,512]{2,1,0:T(8,128)(2,1)S(1)} %pad_maximum_fusion.14), channel_id=1, source_target_pairs={{0,8},{1,9},{4,12},{5,13},{8,0},{9,1},{12,4},{13,5},{2,10},{3,11},... | collective-permute-start | bytes 294920 | tf_op jit(solution)/shard_map/ppermute | solution.py:37
  23.5 34.6 %copy-start.23 = (f32[1,1,512]{2,1,0:T(1,128)}, f32[1,1,512]{2,1,0:T(1,128)S(1)}, u32[]{:S(2)}) copy-start(f32[1,1,512]{2,1,0:T(1,128)S(1)} %get-tuple-element.324) | copy-start | bytes 6148
  23.5 39.4 %copy-start.25 = (f32[1,1,512]{2,1,0:T(1,128)}, f32[1,1,512]{2,1,0:T(1,128)S(1)}, u32[]{:S(2)}) copy-start(f32[1,1,512]{2,1,0:T(1,128)S(1)} %get-tuple-element.326) | copy-start | bytes 6148
  24.7 23.9 %copy-start.71 = (f32[1,1,512]{2,1,0:T(1,128)}, f32[1,1,512]{2,1,0:T(1,128)S(1)}, u32[]{:S(2)}) copy-start(f32[1,1,512]{2,1,0:T(1,128)S(1)} %get-tuple-element.260) | copy-start | bytes 6148
  24.7 23.9 %copy-start.73 = (f32[1,1,512]{2,1,0:T(1,128)}, f32[1,1,512]{2,1,0:T(1,128)S(1)}, u32[]{:S(2)}) copy-start(f32[1,1,512]{2,1,0:T(1,128)S(1)} %get-tuple-element.261) | copy-start | bytes 6148
  24.7 23.9 %copy-start.75 = (f32[1,1,512]{2,1,0:T(1,128)}, f32[1,1,512]{2,1,0:T(1,128)S(1)}, u32[]{:S(2)}) copy-start(f32[1,1,512]{2,1,0:T(1,128)S(1)} %get-tuple-element.262) | copy-start | bytes 6148
  24.8 23.9 %copy-start.77 = (f32[1,1,512]{2,1,0:T(1,128)}, f32[1,1,512]{2,1,0:T(1,128)S(1)}, u32[]{:S(2)}) copy-start(f32[1,1,512]{2,1,0:T(1,128)S(1)} %get-tuple-element.263) | copy-start | bytes 6148
  24.8 23.9 %copy-start.79 = (f32[1,1,512]{2,1,0:T(1,128)}, f32[1,1,512]{2,1,0:T(1,128)S(1)}, u32[]{:S(2)}) copy-start(f32[1,1,512]{2,1,0:T(1,128)S(1)} %get-tuple-element.264) | copy-start | bytes 6148
  24.8 23.9 %copy-start.81 = (f32[1,1,512]{2,1,0:T(1,128)}, f32[1,1,512]{2,1,0:T(1,128)S(1)}, u32[]{:S(2)}) copy-start(f32[1,1,512]{2,1,0:T(1,128)S(1)} %get-tuple-element.265) | copy-start | bytes 6148
  24.8 23.9 %copy-start.83 = (f32[1,1,512]{2,1,0:T(1,128)}, f32[1,1,512]{2,1,0:T(1,128)S(1)}, u32[]{:S(2)}) copy-start(f32[1,1,512]{2,1,0:T(1,128)S(1)} %get-tuple-element.266) | copy-start | bytes 6148
  24.8 23.9 %copy-start.85 = (f32[1,1,512]{2,1,0:T(1,128)}, f32[1,1,512]{2,1,0:T(1,128)S(1)}, u32[]{:S(2)}) copy-start(f32[1,1,512]{2,1,0:T(1,128)S(1)} %get-tuple-element.267) | copy-start | bytes 6148
  24.8 23.9 %copy-start.87 = (f32[1,1,512]{2,1,0:T(1,128)}, f32[1,1,512]{2,1,0:T(1,128)S(1)}, u32[]{:S(2)}) copy-start(f32[1,1,512]{2,1,0:T(1,128)S(1)} %get-tuple-element.268) | copy-start | bytes 6148
  24.8 23.9 %copy-start.89 = (f32[1,1,512]{2,1,0:T(1,128)}, f32[1,1,512]{2,1,0:T(1,128)S(1)}, u32[]{:S(2)}) copy-start(f32[1,1,512]{2,1,0:T(1,128)S(1)} %get-tuple-element.269) | copy-start | bytes 6148
  24.8 23.9 %copy-start.91 = (f32[1,1,512]{2,1,0:T(1,128)}, f32[1,1,512]{2,1,0:T(1,128)S(1)}, u32[]{:S(2)}) copy-start(f32[1,1,512]{2,1,0:T(1,128)S(1)} %get-tuple-element.270) | copy-start | bytes 6148
  24.8 23.9 %copy-start.93 = (f32[1,1,512]{2,1,0:T(1,128)}, f32[1,1,512]{2,1,0:T(1,128)S(1)}, u32[]{:S(2)}) copy-start(f32[1,1,512]{2,1,0:T(1,128)S(1)} %get-tuple-element.271) | copy-start | bytes 6148
  24.8 23.9 %copy-start.95 = (f32[1,1,512]{2,1,0:T(1,128)}, f32[1,1,512]{2,1,0:T(1,128)S(1)}, u32[]{:S(2)}) copy-start(f32[1,1,512]{2,1,0:T(1,128)S(1)} %get-tuple-element.272) | copy-start | bytes 6148
  24.9 23.9 %copy-start.97 = (f32[1,1,512]{2,1,0:T(1,128)}, f32[1,1,512]{2,1,0:T(1,128)S(1)}, u32[]{:S(2)}) copy-start(f32[1,1,512]{2,1,0:T(1,128)S(1)} %get-tuple-element.273) | copy-start | bytes 6148
  24.9 23.9 %copy-start.99 = (f32[1,1,512]{2,1,0:T(1,128)}, f32[1,1,512]{2,1,0:T(1,128)S(1)}, u32[]{:S(2)}) copy-start(f32[1,1,512]{2,1,0:T(1,128)S(1)} %get-tuple-element.274) | copy-start | bytes 6148
  25.5 37.5 %copy-start.29 = (f32[1,1,512]{2,1,0:T(1,128)}, f32[1,1,512]{2,1,0:T(1,128)S(1)}, u32[]{:S(2)}) copy-start(f32[1,1,512]{2,1,0:T(1,128)S(1)} %get-tuple-element.281) | copy-start | bytes 6148
  29.2 15.3 %copy-start.31 = (f32[1,1,512]{2,1,0:T(1,128)}, f32[1,1,512]{2,1,0:T(1,128)S(1)}, u32[]{:S(2)}) copy-start(f32[1,1,512]{2,1,0:T(1,128)S(1)} %get-tuple-element.211) | copy-start | bytes 6148
  29.2 19.6 %copy-start.61 = (f32[1,1,512]{2,1,0:T(1,128)}, f32[1,1,512]{2,1,0:T(1,128)S(1)}, u32[]{:S(2)}) copy-start(f32[1,1,512]{2,1,0:T(1,128)S(1)} %get-tuple-element.226) | copy-start | bytes 6148
  29.2 19.6 %copy-start.63 = (f32[1,1,512]{2,1,0:T(1,128)}, f32[1,1,512]{2,1,0:T(1,128)S(1)}, u32[]{:S(2)}) copy-start(f32[1,1,512]{2,1,0:T(1,128)S(1)} %get-tuple-element.227) | copy-start | bytes 6148
  29.2 19.6 %copy-start.65 = (f32[1,1,512]{2,1,0:T(1,128)}, f32[1,1,512]{2,1,0:T(1,128)S(1)}, u32[]{:S(2)}) copy-start(f32[1,1,512]{2,1,0:T(1,128)S(1)} %get-tuple-element.228) | copy-start | bytes 6148
  29.2 28.6 %copy-start.33 = (f32[1,1,512]{2,1,0:T(1,128)}, f32[1,1,512]{2,1,0:T(1,128)S(1)}, u32[]{:S(2)}) copy-start(f32[1,1,512]{2,1,0:T(1,128)S(1)} %get-tuple-element.212) | copy-start | bytes 6148
  29.2 28.5 %copy-start.35 = (f32[1,1,512]{2,1,0:T(1,128)}, f32[1,1,512]{2,1,0:T(1,128)S(1)}, u32[]{:S(2)}) copy-start(f32[1,1,512]{2,1,0:T(1,128)S(1)} %get-tuple-element.213) | copy-start | bytes 6148
  29.2 28.6 %copy-start.37 = (f32[1,1,512]{2,1,0:T(1,128)}, f32[1,1,512]{2,1,0:T(1,128)S(1)}, u32[]{:S(2)}) copy-start(f32[1,1,512]{2,1,0:T(1,128)S(1)} %get-tuple-element.214) | copy-start | bytes 6148
  29.2 28.6 %copy-start.39 = (f32[1,1,512]{2,1,0:T(1,128)}, f32[1,1,512]{2,1,0:T(1,128)S(1)}, u32[]{:S(2)}) copy-start(f32[1,1,512]{2,1,0:T(1,128)S(1)} %get-tuple-element.215) | copy-start | bytes 6148
  29.2 28.6 %copy-start.41 = (f32[1,1,512]{2,1,0:T(1,128)}, f32[1,1,512]{2,1,0:T(1,128)S(1)}, u32[]{:S(2)}) copy-start(f32[1,1,512]{2,1,0:T(1,128)S(1)} %get-tuple-element.216) | copy-start | bytes 6148
  29.3 28.6 %copy-start.43 = (f32[1,1,512]{2,1,0:T(1,128)}, f32[1,1,512]{2,1,0:T(1,128)S(1)}, u32[]{:S(2)}) copy-start(f32[1,1,512]{2,1,0:T(1,128)S(1)} %get-tuple-element.217) | copy-start | bytes 6148
  29.3 28.6 %copy-start.45 = (f32[1,1,512]{2,1,0:T(1,128)}, f32[1,1,512]{2,1,0:T(1,128)S(1)}, u32[]{:S(2)}) copy-start(f32[1,1,512]{2,1,0:T(1,128)S(1)} %get-tuple-element.218) | copy-start | bytes 6148
  29.3 28.6 %copy-start.47 = (f32[1,1,512]{2,1,0:T(1,128)}, f32[1,1,512]{2,1,0:T(1,128)S(1)}, u32[]{:S(2)}) copy-start(f32[1,1,512]{2,1,0:T(1,128)S(1)} %get-tuple-element.219) | copy-start | bytes 6148
  29.3 28.6 %copy-start.49 = (f32[1,1,512]{2,1,0:T(1,128)}, f32[1,1,512]{2,1,0:T(1,128)S(1)}, u32[]{:S(2)}) copy-start(f32[1,1,512]{2,1,0:T(1,128)S(1)} %get-tuple-element.220) | copy-start | bytes 6148
  29.3 28.6 %copy-start.51 = (f32[1,1,512]{2,1,0:T(1,128)}, f32[1,1,512]{2,1,0:T(1,128)S(1)}, u32[]{:S(2)}) copy-start(f32[1,1,512]{2,1,0:T(1,128)S(1)} %get-tuple-element.221) | copy-start | bytes 6148
  29.3 28.6 %copy-start.53 = (f32[1,1,512]{2,1,0:T(1,128)}, f32[1,1,512]{2,1,0:T(1,128)S(1)}, u32[]{:S(2)}) copy-start(f32[1,1,512]{2,1,0:T(1,128)S(1)} %get-tuple-element.222) | copy-start | bytes 6148
  29.3 28.6 %copy-start.55 = (f32[1,1,512]{2,1,0:T(1,128)}, f32[1,1,512]{2,1,0:T(1,128)S(1)}, u32[]{:S(2)}) copy-start(f32[1,1,512]{2,1,0:T(1,128)S(1)} %get-tuple-element.223) | copy-start | bytes 6148
  29.3 28.6 %copy-start.57 = (f32[1,1,512]{2,1,0:T(1,128)}, f32[1,1,512]{2,1,0:T(1,128)S(1)}, u32[]{:S(2)}) copy-start(f32[1,1,512]{2,1,0:T(1,128)S(1)} %get-tuple-element.224) | copy-start | bytes 6148
  29.3 28.6 %copy-start.59 = (f32[1,1,512]{2,1,0:T(1,128)}, f32[1,1,512]{2,1,0:T(1,128)S(1)}, u32[]{:S(2)}) copy-start(f32[1,1,512]{2,1,0:T(1,128)S(1)} %get-tuple-element.225) | copy-start | bytes 6148
  45.8 29.1 %copy-start.27 = (f32[1,1,512]{2,1,0:T(1,128)}, f32[1,1,512]{2,1,0:T(1,128)S(1)}, u32[]{:S(2)}) copy-start(f32[1,1,512]{2,1,0:T(1,128)S(1)} %get-tuple-element.230) | copy-start | bytes 6148
  49.0 6.0 %collective-permute-start.3 = (bf16[14,3,512]{2,1,0:T(4,128)(2,1)S(1)}, bf16[14,3,512]{2,1,0:T(4,128)(2,1)S(1)}, u32[]{:S(2)}, u32[]{:S(2)}) collective-permute-start(bf16[14,3,512]{2,1,0:T(4,128)(2,1)S(1)} %get-tuple-element.202), channel_id=1, source_target_pairs={{0,1},{1,4},{4,5},{5,8},{8,9},{9,12},{12,13},{13,0},{2,3},{3,6},{6... | collective-permute-start | bytes 129032 | tf_op jit(solution)/shard_map/ppermute | solution.py:25
  49.2 5.8 %collective-permute-start.4 = (bf16[14,3,512]{2,1,0:T(4,128)(2,1)S(1)}, bf16[14,3,512]{2,1,0:T(4,128)(2,1)S(1)}, u32[]{:S(2)}, u32[]{:S(2)}) collective-permute-start(bf16[14,3,512]{2,1,0:T(4,128)(2,1)S(1)} %get-tuple-element.203), channel_id=1, source_target_pairs={{1,0},{4,1},{5,4},{8,5},{9,8},{12,9},{13,12},{0,13},{3,2},{6,3},{7... | collective-permute-start | bytes 129032 | tf_op jit(solution)/shard_map/ppermute | solution.py:27
  63.0 7.7 %collective-permute-start.5 = (bf16[6,16,512]{2,1,0:T(8,128)(2,1)S(1)}, bf16[6,16,512]{2,1,0:T(8,128)(2,1)S(1)}, u32[]{:S(2)}, u32[]{:S(2)}) collective-permute-start(bf16[6,16,512]{2,1,0:T(8,128)(2,1)S(1)} %pad_maximum_fusion.15), channel_id=1, source_target_pairs={{0,8},{1,9},{4,12},{5,13},{8,0},{9,1},{12,4},{13,5},{2,10},{3,11},... | collective-permute-start | bytes 294920 | tf_op jit(solution)/shard_map/ppermute | solution.py:37
  63.7 7.0 %collective-permute-start.7 = (bf16[3,16,512]{2,1,0:T(8,128)(2,1)S(1)}, bf16[3,16,512]{2,1,0:T(8,128)(2,1)S(1)}, u32[]{:S(2)}, u32[]{:S(2)}) collective-permute-start(bf16[3,16,512]{2,1,0:T(8,128)(2,1)S(1)} %get-tuple-element.209), channel_id=1, source_target_pairs={{2,0},{3,1},{6,4},{7,5},{10,8},{11,9},{14,12},{15,13},{18,16},{19,... | collective-permute-start | bytes 147464 | tf_op jit(solution)/shard_map/ppermute | solution.py:27
  65.0 6.3 %collective-permute-start.6 = (bf16[3,16,512]{2,1,0:T(8,128)(2,1)S(1)}, bf16[3,16,512]{2,1,0:T(8,128)(2,1)S(1)}, u32[]{:S(2)}, u32[]{:S(2)}) collective-permute-start(bf16[3,16,512]{2,1,0:T(8,128)(2,1)S(1)} %get-tuple-element.208), channel_id=1, source_target_pairs={{0,2},{1,3},{4,6},{5,7},{8,10},{9,11},{12,14},{13,15},{16,18},{17,... | collective-permute-start | bytes 147464 | tf_op jit(solution)/shard_map/ppermute | solution.py:25
  71.3 5.6 %collective-permute-start.8 = (bf16[14,3,512]{2,1,0:T(4,128)(2,1)S(1)}, bf16[14,3,512]{2,1,0:T(4,128)(2,1)S(1)}, u32[]{:S(2)}, u32[]{:S(2)}) collective-permute-start(bf16[14,3,512]{2,1,0:T(4,128)(2,1)S(1)} %get-tuple-element.198), channel_id=1, source_target_pairs={{0,1},{1,4},{4,5},{5,8},{8,9},{9,12},{12,13},{13,0},{2,3},{3,6},{6... | collective-permute-start | bytes 129032 | tf_op jit(solution)/shard_map/ppermute | solution.py:25
  71.4 5.6 %collective-permute-start.9 = (bf16[14,3,512]{2,1,0:T(4,128)(2,1)S(1)}, bf16[14,3,512]{2,1,0:T(4,128)(2,1)S(1)}, u32[]{:S(2)}, u32[]{:S(2)}) collective-permute-start(bf16[14,3,512]{2,1,0:T(4,128)(2,1)S(1)} %get-tuple-element.199), channel_id=1, source_target_pairs={{1,0},{4,1},{5,4},{8,5},{9,8},{12,9},{13,12},{0,13},{3,2},{6,3},{7... | collective-permute-start | bytes 129032 | tf_op jit(solution)/shard_map/ppermute | solution.py:27
  86.1 25.8 %collective-permute-start.13 = (bf16[3,16,512]{2,1,0:T(8,128)(2,1)S(1)}, bf16[3,16,512]{2,1,0:T(8,128)(2,1)}, u32[]{:S(2)}, u32[]{:S(2)}) collective-permute-start(bf16[3,16,512]{2,1,0:T(8,128)(2,1)S(1)} %get-tuple-element.207), channel_id=1, source_target_pairs={{2,0},{3,1},{6,4},{7,5},{10,8},{11,9},{14,12},{15,13},{18,16},{19,... | collective-permute-start | bytes 147464 | tf_op jit(solution)/shard_map/ppermute | solution.py:27
  87.5 25.3 %collective-permute-start.12 = (bf16[3,16,512]{2,1,0:T(8,128)(2,1)S(1)}, bf16[3,16,512]{2,1,0:T(8,128)(2,1)}, u32[]{:S(2)}, u32[]{:S(2)}) collective-permute-start(bf16[3,16,512]{2,1,0:T(8,128)(2,1)S(1)} %get-tuple-element.206), channel_id=1, source_target_pairs={{0,2},{1,3},{4,6},{5,7},{8,10},{9,11},{12,14},{13,15},{16,18},{17,... | collective-permute-start | bytes 147464 | tf_op jit(solution)/shard_map/ppermute | solution.py:25
  95.7 20.7 %collective-permute-start.10 = (bf16[8,16,512]{2,1,0:T(8,128)(2,1)}, bf16[8,16,512]{2,1,0:T(8,128)(2,1)S(1)}, u32[]{:S(2)}, u32[]{:S(2)}) collective-permute-start(bf16[8,16,512]{2,1,0:T(8,128)(2,1)} %get-tuple-element.526), channel_id=1, source_target_pairs={{0,1},{1,0},{2,3},{3,2},{4,5},{5,4},{6,7},{7,6},{8,9},{9,8},{10,11... | collective-permute-start | bytes 393224 | tf_op jit(solution)/shard_map/ppermute | solution.py:41
  95.8 16.1 %collective-permute-start.11 = (bf16[6,16,512]{2,1,0:T(8,128)(2,1)S(1)}, bf16[6,16,512]{2,1,0:T(8,128)(2,1)S(1)}, u32[]{:S(2)}, u32[]{:S(2)}) collective-permute-start(bf16[6,16,512]{2,1,0:T(8,128)(2,1)S(1)} %pad_maximum_fusion.16), channel_id=1, source_target_pairs={{0,8},{1,9},{4,12},{5,13},{8,0},{9,1},{12,4},{13,5},{2,10},{3,11},... | collective-permute-start | bytes 294920 | tf_op jit(solution)/shard_map/ppermute | solution.py:37
  112.9 5.5 %collective-permute-start.14 = (bf16[14,3,512]{2,1,0:T(4,128)(2,1)S(1)}, bf16[14,3,512]{2,1,0:T(4,128)(2,1)S(1)}, u32[]{:S(2)}, u32[]{:S(2)}) collective-permute-start(bf16[14,3,512]{2,1,0:T(4,128)(2,1)S(1)} %get-tuple-element.194), channel_id=1, source_target_pairs={{0,1},{1,4},{4,5},{5,8},{8,9},{9,12},{12,13},{13,0},{2,3},{3,6},{6... | collective-permute-start | bytes 129032 | tf_op jit(solution)/shard_map/ppermute | solution.py:25
  113.1 5.3 %collective-permute-start.15 = (bf16[14,3,512]{2,1,0:T(4,128)(2,1)S(1)}, bf16[14,3,512]{2,1,0:T(4,128)(2,1)S(1)}, u32[]{:S(2)}, u32[]{:S(2)}) collective-permute-start(bf16[14,3,512]{2,1,0:T(4,128)(2,1)S(1)} %get-tuple-element.195), channel_id=1, source_target_pairs={{1,0},{4,1},{5,4},{8,5},{9,8},{12,9},{13,12},{0,13},{3,2},{6,3},{7... | collective-permute-start | bytes 129032 | tf_op jit(solution)/shard_map/ppermute | solution.py:27
  129.6 97.4 %collective-permute-start.18 = (bf16[3,16,512]{2,1,0:T(8,128)(2,1)S(1)}, bf16[3,16,512]{2,1,0:T(8,128)(2,1)}, u32[]{:S(2)}, u32[]{:S(2)}) collective-permute-start(bf16[3,16,512]{2,1,0:T(8,128)(2,1)S(1)} %get-tuple-element.205), channel_id=1, source_target_pairs={{2,0},{3,1},{6,4},{7,5},{10,8},{11,9},{14,12},{15,13},{18,16},{19,... | collective-permute-start | bytes 147464 | tf_op jit(solution)/shard_map/ppermute | solution.py:27
  131.6 96.3 %collective-permute-start.17 = (bf16[3,16,512]{2,1,0:T(8,128)(2,1)S(1)}, bf16[3,16,512]{2,1,0:T(8,128)(2,1)}, u32[]{:S(2)}, u32[]{:S(2)}) collective-permute-start(bf16[3,16,512]{2,1,0:T(8,128)(2,1)S(1)} %get-tuple-element.204), channel_id=1, source_target_pairs={{0,2},{1,3},{4,6},{5,7},{8,10},{9,11},{12,14},{13,15},{16,18},{17,... | collective-permute-start | bytes 147464 | tf_op jit(solution)/shard_map/ppermute | solution.py:25
  140.4 85.7 %collective-permute-start.16 = (bf16[6,16,512]{2,1,0:T(8,128)(2,1)}, bf16[6,16,512]{2,1,0:T(8,128)(2,1)}, u32[]{:S(2)}, u32[]{:S(2)}) collective-permute-start(bf16[6,16,512]{2,1,0:T(8,128)(2,1)} %pad_maximum_fusion.17), channel_id=1, source_target_pairs={{0,8},{1,9},{4,12},{5,13},{8,0},{9,1},{12,4},{13,5},{2,10},{3,11},... | collective-permute-start | bytes 294920 | tf_op jit(solution)/shard_map/ppermute | solution.py:37
  228.2 6.0 %collective-permute-start.19 = (bf16[14,3,512]{2,1,0:T(4,128)(2,1)S(1)}, bf16[14,3,512]{2,1,0:T(4,128)(2,1)S(1)}, u32[]{:S(2)}, u32[]{:S(2)}) collective-permute-start(bf16[14,3,512]{2,1,0:T(4,128)(2,1)S(1)} %get-tuple-element.190), channel_id=1, source_target_pairs={{0,1},{1,4},{4,5},{5,8},{8,9},{9,12},{12,13},{13,0},{2,3},{3,6},{6... | collective-permute-start | bytes 129032 | tf_op jit(solution)/shard_map/ppermute | solution.py:25
  228.2 5.9 %collective-permute-start.20 = (bf16[14,3,512]{2,1,0:T(4,128)(2,1)S(1)}, bf16[14,3,512]{2,1,0:T(4,128)(2,1)S(1)}, u32[]{:S(2)}, u32[]{:S(2)}) collective-permute-start(bf16[14,3,512]{2,1,0:T(4,128)(2,1)S(1)} %get-tuple-element.191), channel_id=1, source_target_pairs={{1,0},{4,1},{5,4},{8,5},{9,8},{12,9},{13,12},{0,13},{3,2},{6,3},{7... | collective-permute-start | bytes 129032 | tf_op jit(solution)/shard_map/ppermute | solution.py:27
  240.7 1.4 collective-permute-start.21
  (148 other events, 739.1 us)
Sparse Core Ops, SparseCore 0:
  9.5 16.4 all-gather.4
  27.6 14.7 all-gather.6

commit v2 on v1

--- a/solution.py
+++ b/solution.py
@@ -50,6 +50,22 @@
             )
             accumulated = accumulated + window * stencil[row_tap, col_tap].astype(jnp.float32)
     return accumulated
+
+
+def edge_terms(rows, stencil, first_tap, out_cols):
+    margin = rows.shape[0]
+    terms = []
+    for out_row in range(margin):
+        total = jnp.zeros((out_cols, rows.shape[2]), jnp.float32)
+        for row in range(margin):
+            tap = first_tap + row - out_row
+            if tap < 0 or tap >= KERNEL:
+                continue
+            for col_tap in range(KERNEL):
+                window = rows[row, col_tap : col_tap + out_cols].astype(jnp.float32)
+                total = total + window * stencil[tap, col_tap]
+        terms.append(total)
+    return jnp.stack(terms)
 
 
 def stencil_terms(padded, grad_low, out_rows, out_cols):
@@ -149,11 +165,8 @@
     flipped = stencil_grid[::-1, ::-1]
     correction = stencil_grid[:, ::-1] - flipped
     through = correlate(spread, flipped, out_rows, out_cols)
-    zero_rows = jnp.zeros_like(spread[: 2 * margin])
-    top_part = jnp.concatenate([spread[:margin], zero_rows], axis=0)
-    bottom_part = jnp.concatenate([zero_rows, spread[-margin:]], axis=0)
-    top_fix = correlate(top_part, correction, margin, out_cols) * north_weight
-    bottom_fix = correlate(bottom_part, correction, margin, out_cols) * south_weight
+    top_fix = edge_terms(spread[:margin], correction, 0, out_cols) * north_weight
+    bottom_fix = edge_terms(spread[-margin:], correction, KERNEL - 1, out_cols) * south_weight
     rest_rows = out_rows - margin
     top_full = jnp.pad(top_fix, ((0, rest_rows), (0, 0), (0, 0)))
     bottom_full = jnp.pad(bottom_fix, ((rest_rows, 0), (0, 0), (0, 0)))
@@ -182,17 +195,93 @@
     return partner_2(values, "segment", 0)
 
 
+def halo_kernel(rows_ref, cols_ref, nooks_ref, rows_out, cols_out, nooks_out, send_sem, recv_sem):
+    lon, lat, core = lax.axis_index("lon"), lax.axis_index("lat"), lax.axis_index("segment")
+    lats, cores = lax.axis_size("lat"), lax.axis_size("segment")
+    count = lax.axis_size("lon") * cores
+    spot = lon * cores + core
+    first = (lats - lat) // lats
+    last = (lat + 1) // lats
+
+    def device(row, column):
+        column = (column + count) % count
+        return {"lat": row, "lon": column // cores, "segment": column % cores}
+
+    edges = (
+        (0, lat - 1 + first, spot + first * (count // 2), 1 - first),
+        (1, lat + 1 - last, spot + last * (count // 2), last),
+    )
+    moves = []
+    for side, step in ((0, -1), (1, 1)):
+        moves.append((cols_ref.at[side], cols_out.at[1 - side], side, 1 - side, lat, spot + step))
+    for edge, row, column, slot in edges:
+        moves.append((rows_ref.at[edge], rows_out.at[slot], 2 + edge, 2 + slot, row, column))
+        for side, step in ((0, -1), (1, 1)):
+            moves.append(
+                (
+                    nooks_ref.at[edge, side],
+                    nooks_out.at[slot, 1 - side],
+                    4 + 2 * edge + side,
+                    4 + 2 * slot + 1 - side,
+                    row,
+                    column + step,
+                )
+            )
+    barrier = pltpu.get_barrier_semaphore()
+    for move in moves:
+        pl.semaphore_signal(
+            barrier,
+            inc=1,
+            device_id=device(move[4], move[5]),
+            device_id_type=pl.DeviceIdType.MESH,
+        )
+    pl.semaphore_wait(barrier, len(moves))
+    copies = [
+        pltpu.make_async_remote_copy(
+            src_ref=source,
+            dst_ref=target,
+            send_sem=send_sem.at[sent],
+            recv_sem=recv_sem.at[landed],
+            device_id=device(row, column),
+            device_id_type=pl.DeviceIdType.MESH,
+        )
+        for source, target, sent, landed, row, column in moves
+    ]
+    for copy in copies:
+        copy.start()
+    for copy in copies:
+        copy.wait_send()
+    for index in range(2):
+        for source, landed in ((cols_out, index), (rows_out, 2 + index)):
+            pltpu.make_async_copy(source.at[index], source.at[index], recv_sem.at[landed]).wait()
+        for side in range(2):
+            spot_ref = nooks_out.at[index, side]
+            pltpu.make_async_copy(spot_ref, spot_ref, recv_sem.at[4 + 2 * index + side]).wait()
+
+
 def extend_local(values, northern, southern, row_source):
     margin = KERNEL // 2
-    edge_rows = jnp.concatenate([values[:margin], values[-margin:]], axis=0)
-    nearby = row_source(edge_rows)
-    partner = pole_partner(edge_rows)
-    upper_rows = jnp.where(northern, partner[:margin][::-1], nearby[:margin])
-    lower_rows = jnp.where(southern, partner[margin:][::-1], nearby[-margin:])
-    lat_extended = jnp.concatenate([upper_rows, values, lower_rows], axis=0)
-    edge_cols = jnp.concatenate([lat_extended[:, :margin], lat_extended[:, -margin:]], axis=1)
-    beside_all = lon_neighbours(edge_cols)
-    return jnp.concatenate([beside_all[:, :margin], lat_extended, beside_all[:, -margin:]], axis=1)
+    edge_rows = jnp.stack([values[:margin], values[-margin:]])
+    edge_cols = jnp.stack([values[:, :margin], values[:, -margin:]])
+    nooks = jnp.stack([edge_rows[:, :, :margin], edge_rows[:, :, -margin:]], axis=1)
+    vmem = pl.BlockSpec(memory_space=pltpu.VMEM)
+    sent = (edge_rows, edge_cols, nooks)
+    rows, cols, nooks = pl.pallas_call(
+        halo_kernel,
+        out_shape=[jax.ShapeDtypeStruct(value.shape, value.dtype) for value in sent],
+        in_specs=[vmem] * 3,
+        out_specs=[vmem] * 3,
+        scratch_shapes=[pltpu.SemaphoreType.DMA((8,)), pltpu.SemaphoreType.DMA((8,))],
+        compiler_params=pltpu.CompilerParams(
+            collective_id=1, has_side_effects=True, vmem_limit_bytes=16 * 1024 * 1024
+        ),
+    )(*sent)
+    upper = jnp.concatenate([nooks[0, 0], rows[0], nooks[0, 1]], axis=1)
+    lower = jnp.concatenate([nooks[1, 0], rows[1], nooks[1, 1]], axis=1)
+    upper = jnp.where(northern, upper[::-1], upper)
+    lower = jnp.where(southern, lower[::-1], lower)
+    middle = jnp.concatenate([cols[0], values, cols[1]], axis=1)
+    return jnp.concatenate([upper, middle, lower], axis=0)
 
 
 def both_halves(leading, first, second, dim):

time: 252 us -> 264 us (1.048)
  starting transfers between devices: 45.7 us -> 0.49 us
  local copies, waits for them, and re-layouts: 31.3 us -> 74.1 us
  Pallas kernels: 70.9 us -> 106 us
  other arithmetic: 51.7 us -> 38.8 us
  waiting for transfers between devices: 7.61 us -> 3.41 us
  matrix products: 22.2 us -> 18.4 us
    ppermute x20 -> x0, starting transfers between devices: 45.5 us -> none  [the longest x8 21.5 us: extended(): lax.ppermute(tail, axis, [(i, (i + 1) % count) for i in range(ends)])]
    concatenate x110, local copies, waits for them, and re-layouts: 10.2 us -> 54.1 us  [packed(): rows = jnp.concatenate([stencil_sum, vectors, bias_rows], axis=0)]
    pallas_call x0 -> x4, Pallas kernels: none -> 36.3 us  [extend_local(): pl.pallas_call(halo_kernel, out_shape=[jax.ShapeDtypeStruct(value.shape,...]
    another operation x22 -> x16, other arithmetic: 14.9 us -> 0.53 us  [the longest x8 0.29 us: extend_local(): jnp.stack([edge_rows[:, :, :margin], edge_rows[:, :, -margin:]], axis=1)]
    ppermute x20 -> x0, waiting for transfers between devices: 6.13 us -> none  [the longest x8 4.93 us: extended(): lax.ppermute(tail, axis, [(i, (i + 1) % count) for i in range(ends)])]
    mul x4, other arithmetic: 4.65 us -> 0.03 us  [the longest x2 0.02 us: backward_section(): edge_terms(spread[:margin], correction, 0, out_cols) * north_weight]
    slice x8 -> x6, local copies, waits for them, and re-layouts: 0.89 us -> 3.92 us  [edge_terms(): total = total + window * stencil[tap, col_tap]]
    slice x10 -> x6, local copies, waits for them, and re-layouts: 6.5 us -> 3.96 us  [correlate(): stencil[row_tap, col_tap].astype(jnp.float32)]
  transfers between devices with their start and end apart: 24 -> 4, of which waited for: 7 -> 1; matrix products, arithmetic and copies ran while one was open for 29% -> 36% of each run, Pallas kernels for 28% -> 34%
where the time goes in v2:
time: 264 us; the launch traced here: 263 us
  Pallas kernels  106 us (40%)
  local copies, waits for them, and re-layouts  74.1 us (28%)
  other arithmetic  38.8 us (15%)
  matrix products  18.4 us (7%)
  between operations  17.4 us (7%)
  blocking collectives  3.88 us (1%)
  waiting for transfers between devices  3.41 us (1%)
    pallas_call x1, Pallas kernels, reduced(): pl.pallas_call(functools.partial(reduce_kernel, orders, depth), out_shape...  70 us
    concatenate x110, local copies, waits for them, and re-layouts, packed(): rows = jnp.concatenate([stencil_sum, vectors, bias_rows], axis=0)  54.1 us
    pallas_call x4, Pallas kernels, extend_local(): pl.pallas_call(halo_kernel, out_shape=[jax.ShapeDtypeStruct(value.shape,...  36.3 us
    reduce_sum x8, other arithmetic, stencil_terms(): columns.append(jnp.sum(window * grad_wide, axis=(0, 1)))  8.3 us
  transfers between devices with their start and end apart: 4, of which 1 were waited for; matrix products, arithmetic and copies ran while one was open for 36% of the time, Pallas kernels for 34%

profile of v2, /device:TPU:0, one launch (start us, length us, event | category | flops | bytes accessed | tf_op | source)
XLA Modules:
  0.0 262.8 jit_solution(12560535062596602996)
XLA Ops:
  8.9 2.0 all_gather.17
  12.4 1.9 all-gather.1
  15.1 10.9 %shard_map.162 = (bf16[2,3,16,512]{3,2,1,0:T(8,128)(2,1)S(1)}, bf16[2,8,3,512]{3,2,1,0:T(4,128)(2,1)S(1)}, bf16[2,2,3,3,512]{4,3,2,1,0:T(4,128)(2,1)S(1)}) custom-call(bf16[2,3,16,512]{3,2,1,0:T(8,128)(2,1)S(1)} %pad_maximum_fusion.12.rows_ref, bf16[2,8,3,512]{3,2,1,0:T(4,128)(2,1)S(1)} %pad_maximum_fusion.24.cols_ref, ...), custom_call_target="tpu_custom_call" | custom-call | tf_op jit(solution)/shard_map/pallas_call | solution.py:269
  26.3 2.6 fusion.484
  38.1 2.2 convolution_add_fusion.1
  40.4 2.0 all-gather.7.cloned.1.call-done
  42.4 2.1 fusion.15
  44.8 9.5 %shard_map.163 = (bf16[2,3,16,512]{3,2,1,0:T(8,128)(2,1)S(1)}, bf16[2,8,3,512]{3,2,1,0:T(4,128)(2,1)S(1)}, bf16[2,2,3,3,512]{4,3,2,1,0:T(4,128)(2,1)S(1)}) custom-call(bf16[2,3,16,512]{3,2,1,0:T(8,128)(2,1)S(1)} %pad_maximum_fusion.13.rows_ref, bf16[2,8,3,512]{3,2,1,0:T(4,128)(2,1)S(1)} %pad_maximum_fusion.25.cols_ref, ...), custom_call_target="tpu_custom_call" | custom-call | tf_op jit(solution)/shard_map/pallas_call | solution.py:269
  54.6 2.6 fusion.482
  58.4 1.0 fusion.294
  59.4 1.3 fusion.476
  60.7 2.4 fusion.474
  63.1 1.5 multiply_reduce_fusion
  65.9 8.3 %shard_map.164 = (bf16[2,3,16,512]{3,2,1,0:T(8,128)(2,1)S(1)}, bf16[2,8,3,512]{3,2,1,0:T(4,128)(2,1)S(1)}, bf16[2,2,3,3,512]{4,3,2,1,0:T(4,128)(2,1)S(1)}) custom-call(bf16[2,3,16,512]{3,2,1,0:T(8,128)(2,1)S(1)} %pad_maximum_fusion.14.rows_ref, bf16[2,8,3,512]{3,2,1,0:T(4,128)(2,1)S(1)} %pad_maximum_fusion.26.cols_ref, ...), custom_call_target="tpu_custom_call" | custom-call | tf_op jit(solution)/shard_map/pallas_call | solution.py:269
  74.9 0.8 fusion.361
  75.9 0.8 fusion.327
  77.0 3.7 %fusion.295 = (bf16[512]{0:T(512)(128)(2,1)}, bf16[8,16,512]{2,1,0:T(8,128)(2,1)S(1)}) fusion(f32[128,512]{1,0:T(8,128)S(1)} %fusion.15, f32[3,16,512]{2,1,0:T(8,128)S(1)} %maximum_multiply_fusion.1, f32[3,16,512]{2,1,0:T(8,128)S(1)} %maximum_multiply_fusion, f32[512]{0:T(512)S(1)} %bitcast.799, bf16[11,22,512]{2,1,0:T(8,128)(2,1)S(1)} %get-tuple-element.217, ...), kind=kLoop, calls=%fused_computation.527 | loop fusion | flops 11271680 | bytes 6507524 | tf_op jit(solution)/shard_map/reduce_sum | solution.py:141
  81.3 1.8 fusion.478
  83.1 1.5 multiply_reduce_fusion.1
  86.2 1.2 fusion.265
  87.3 1.1 fusion.292
  88.4 1.2 fusion.293
  90.3 1.2 fusion.191
  91.5 1.1 fusion.218
  92.7 1.2 fusion.219
  94.2 7.6 %shard_map.165 = (bf16[2,3,16,512]{3,2,1,0:T(8,128)(2,1)S(1)}, bf16[2,8,3,512]{3,2,1,0:T(4,128)(2,1)S(1)}, bf16[2,2,3,3,512]{4,3,2,1,0:T(4,128)(2,1)S(1)}) custom-call(bf16[2,3,16,512]{3,2,1,0:T(8,128)(2,1)S(1)} %pad_maximum_fusion.15.rows_ref, bf16[2,8,3,512]{3,2,1,0:T(4,128)(2,1)S(1)} %pad_maximum_fusion.27.cols_ref, ...), custom_call_target="tpu_custom_call" | custom-call | tf_op jit(solution)/shard_map/pallas_call | solution.py:269
  102.6 0.8 fusion.409
  103.8 0.8 fusion.375
  104.9 3.7 %select_bitcast_fusion = (bf16[1,8,16,512]{3,2,1,0:T(8,128)(2,1)}, bf16[8,16,512]{2,1,0:T(8,128)(2,1)S(1)}) fusion(bf16[8,16,512]{2,1,0:T(8,128)(2,1)S(1)} %get-tuple-element.193, pred[]{:T(512)S(6)} %eq.9, f32[3,16,512]{2,1,0:T(8,128)S(1)} %maximum_multiply_fusion.3, f32[3,16,512]{2,1,0:T(8,128)S(1)} %maximum_multiply_fusion.2, f32[512]{0:T(512)S(1)} %bitcast.734, ...), kind=kLoop, calls=%fused_computation.604 | loop fusion | flops 11141120 | bytes 6375425 | tf_op jit(solution)/shard_map/concatenate | solution.py:292
  109.7 1.3 fusion.47
  111.1 1.3 copy.267
  112.7 0.8 concatenate.688
  131.4 1.4 concatenate.738
  132.7 1.3 concatenate.739
  134.7 1.3 concatenate.741
  136.1 0.8 reshape.1695
  136.8 2.5 fusion.43
  139.7 1.3 copy.269
  142.7 0.8 concatenate.744
  144.2 0.8 concatenate.746
  146.5 0.8 concatenate.749
  150.9 0.8 concatenate.755
  153.1 0.8 concatenate.758
  153.9 0.8 concatenate.759
  156.1 0.8 concatenate.762
  156.9 0.8 concatenate.763
  157.7 0.8 concatenate.764
  161.5 0.8 concatenate.770
  162.2 0.8 concatenate.771
  163.0 0.8 concatenate.772
  164.5 0.8 concatenate.774
  166.0 0.8 concatenate.776
  166.8 0.8 concatenate.777
  168.7 0.8 concatenate.792
  169.5 0.8 concatenate.793
  170.3 0.8 concatenate.795
  171.1 0.8 reshape.1700
  174.8 2.0 convolution_convert_fusion.1
  176.8 2.0 convolution_convert_fusion
  178.8 70.0 %shard_map.166 = (f32[256,512]{1,0:T(8,128)S(1)}, f32[256,512]{1,0:T(8,128)S(1)}, f32[64,128]{1,0:T(8,128)S(1)}) custom-call(bf16[2,2,2,256,512]{4,3,2,1,0:T(8,128)(2,1)S(1)} %bitcast.548, bf16[2,2,2,256,512]{4,3,2,1,0:T(8,128)(2,1)S(1)} %bitcast.549, bf16[2,2,2,64,128]{4,3,2,1,0:T(8,128)(2,1)S(1)} %bitcast.550, bf16[2,2,2,256,512]{4,3,2,1,0:T(8,128)(2,1)} %bitcast.554, ...), custom_call_target="tpu_custom_call" | custom-call | tf_op jit(solution)/shard_map/pallas_call | solution.py:472
  248.8 1.0 copy.264
  251.7 1.8 maximum_select_fusion
  253.4 1.8 maximum_select_fusion.1
  255.2 0.8 copy.274
  (649 shorter events, 61.0 us)
Async XLA Ops:
  7.2 30.9 %all-gather.5.cloned.1.call-start = ((), (), s32[]{:S(2)}) async-start(), calls=%async_computation | async-start | bytes 6291456 | tf_op jit(solution)/shard_map/all_gather | solution.py:534
  8.0 34.4 %all-gather.7.cloned.1.call-start = ((), (), s32[]{:S(2)}) async-start(), calls=%async_computation.1 | async-start | bytes 6291456 | tf_op jit(solution)/shard_map/all_gather | solution.py:534
  14.9 23.1 %copy-start.41 = (f32[1,1,512]{2,1,0:T(1,128)}, f32[1,1,512]{2,1,0:T(1,128)S(1)}, u32[]{:S(2)}) copy-start(f32[1,1,512]{2,1,0:T(1,128)S(1)} %get-tuple-element.346) | copy-start | bytes 6148
  14.9 29.6 %copy-start.43 = (f32[1,1,512]{2,1,0:T(1,128)}, f32[1,1,512]{2,1,0:T(1,128)S(1)}, u32[]{:S(2)}) copy-start(f32[1,1,512]{2,1,0:T(1,128)S(1)} %get-tuple-element.348) | copy-start | bytes 6148
  14.9 42.5 %copy-start.59 = (f32[1,1,512]{2,1,0:T(1,128)}, f32[1,1,512]{2,1,0:T(1,128)S(1)}, u32[]{:S(2)}) copy-start(f32[1,1,512]{2,1,0:T(1,128)S(1)} %get-tuple-element.342) | copy-start | bytes 6148
  28.9 11.5 %copy-start.8 = (f32[8,16]{1,0:T(8,128)}, f32[8,16]{1,0:T(8,128)S(1)}, u32[]{:S(2)}) copy-start(f32[8,16]{1,0:T(8,128)S(1)} %broadcast_multiply_fusion.5) | copy-start | bytes 1540
  94.0 157.7 %collective-permute-start = (bf16[8,16,512]{2,1,0:T(8,128)(2,1)}, bf16[8,16,512]{2,1,0:T(8,128)(2,1)}, u32[]{:S(2)}, u32[]{:S(2)}) collective-permute-start(bf16[8,16,512]{2,1,0:T(8,128)(2,1)} %get-tuple-element.568), channel_id=1, source_target_pairs={{0,1},{1,0},{2,3},{3,2},{4,5},{5,4},{6,7},{7,6},{8,9},{9,8},{10,11... | collective-permute-start | bytes 393224 | tf_op jit(solution)/shard_map/ppermute | solution.py:41
  109.3 144.2 %collective-permute-start.1 = (bf16[8,16,512]{2,1,0:T(8,128)(2,1)}, bf16[8,16,512]{2,1,0:T(8,128)(2,1)}, u32[]{:S(2)}, u32[]{:S(2)}) collective-permute-start(bf16[8,16,512]{2,1,0:T(8,128)(2,1)} %broadcast_select_fusion), channel_id=1, source_target_pairs={{0,1},{1,0},{2,3},{3,2},{4,5},{5,4},{6,7},{7,6},{8,9},{9,8},{10,11... | collective-permute-start | bytes 393224 | tf_op jit(solution)/shard_map/ppermute | solution.py:41
  109.6 21.0 %copy-start.151 = (bf16[512]{0:T(512)(128)(2,1)S(1)}, bf16[512]{0:T(512)(128)(2,1)}, u32[]{:S(2)}) copy-start(bf16[512]{0:T(512)(128)(2,1)} %get-tuple-element.196) | copy-start | bytes 3076
  109.7 24.4 %copy-start.147 = (bf16[512]{0:T(512)(128)(2,1)S(1)}, bf16[512]{0:T(512)(128)(2,1)}, u32[]{:S(2)}) copy-start(bf16[512]{0:T(512)(128)(2,1)} %get-tuple-element.194) | copy-start | bytes 3076
  111.0 11.6 %copy-start.174 = (bf16[512]{0:T(512)(128)(2,1)S(1)}, bf16[512]{0:T(512)(128)(2,1)}, u32[]{:S(2)}) copy-start(bf16[512]{0:T(512)(128)(2,1)} %get-tuple-element.114) | copy-start | bytes 3076
  111.0 12.2 %copy-start.173 = (bf16[512]{0:T(512)(128)(2,1)S(1)}, bf16[512]{0:T(512)(128)(2,1)}, u32[]{:S(2)}) copy-start(bf16[512]{0:T(512)(128)(2,1)} %get-tuple-element.115) | copy-start | bytes 3076
  111.0 12.9 %copy-start.172 = (bf16[512]{0:T(512)(128)(2,1)S(1)}, bf16[512]{0:T(512)(128)(2,1)}, u32[]{:S(2)}) copy-start(bf16[512]{0:T(512)(128)(2,1)} %get-tuple-element.116) | copy-start | bytes 3076
  111.0 13.6 %copy-start.171 = (bf16[512]{0:T(512)(128)(2,1)S(1)}, bf16[512]{0:T(512)(128)(2,1)}, u32[]{:S(2)}) copy-start(bf16[512]{0:T(512)(128)(2,1)} %get-tuple-element.117) | copy-start | bytes 3076
  111.1 14.2 %copy-start.170 = (bf16[512]{0:T(512)(128)(2,1)S(1)}, bf16[512]{0:T(512)(128)(2,1)}, u32[]{:S(2)}) copy-start(bf16[512]{0:T(512)(128)(2,1)} %get-tuple-element.118) | copy-start | bytes 3076
  111.1 14.9 %copy-start.169 = (bf16[512]{0:T(512)(128)(2,1)S(1)}, bf16[512]{0:T(512)(128)(2,1)}, u32[]{:S(2)}) copy-start(bf16[512]{0:T(512)(128)(2,1)} %get-tuple-element.119) | copy-start | bytes 3076
  111.1 15.6 %copy-start.168 = (bf16[512]{0:T(512)(128)(2,1)S(1)}, bf16[512]{0:T(512)(128)(2,1)}, u32[]{:S(2)}) copy-start(bf16[512]{0:T(512)(128)(2,1)} %get-tuple-element.120) | copy-start | bytes 3076
  111.1 16.2 %copy-start.167 = (bf16[512]{0:T(512)(128)(2,1)S(1)}, bf16[512]{0:T(512)(128)(2,1)}, u32[]{:S(2)}) copy-start(bf16[512]{0:T(512)(128)(2,1)} %get-tuple-element.121) | copy-start | bytes 3076
  111.1 16.9 %copy-start.165 = (bf16[512]{0:T(512)(128)(2,1)S(1)}, bf16[512]{0:T(512)(128)(2,1)}, u32[]{:S(2)}) copy-start(bf16[512]{0:T(512)(128)(2,1)} %get-tuple-element.123) | copy-start | bytes 3076
  111.1 17.6 %copy-start.164 = (bf16[512]{0:T(512)(128)(2,1)S(1)}, bf16[512]{0:T(512)(128)(2,1)}, u32[]{:S(2)}) copy-start(bf16[512]{0:T(512)(128)(2,1)} %get-tuple-element.124) | copy-start | bytes 3076
  111.1 18.2 %copy-start.163 = (bf16[512]{0:T(512)(128)(2,1)S(1)}, bf16[512]{0:T(512)(128)(2,1)}, u32[]{:S(2)}) copy-start(bf16[512]{0:T(512)(128)(2,1)} %get-tuple-element.122) | copy-start | bytes 3076
  111.1 18.9 %copy-start.166 = (bf16[512]{0:T(512)(128)(2,1)S(1)}, bf16[512]{0:T(512)(128)(2,1)}, u32[]{:S(2)}) copy-start(bf16[512]{0:T(512)(128)(2,1)} %get-tuple-element.104) | copy-start | bytes 3076
  139.3 22.0 %copy-start.162 = (bf16[512]{0:T(512)(128)(2,1)S(1)}, bf16[512]{0:T(512)(128)(2,1)}, u32[]{:S(2)}) copy-start(bf16[512]{0:T(512)(128)(2,1)} %get-tuple-element.176) | copy-start | bytes 3076
  139.3 28.2 %copy-start.161 = (bf16[512]{0:T(512)(128)(2,1)S(1)}, bf16[512]{0:T(512)(128)(2,1)}, u32[]{:S(2)}) copy-start(bf16[512]{0:T(512)(128)(2,1)} %get-tuple-element.71) | copy-start | bytes 3076
  139.3 28.3 %copy-start.160 = (bf16[512]{0:T(512)(128)(2,1)S(1)}, bf16[512]{0:T(512)(128)(2,1)}, u32[]{:S(2)}) copy-start(bf16[512]{0:T(512)(128)(2,1)} %get-tuple-element.72) | copy-start | bytes 3076
  139.3 28.4 %copy-start.159 = (bf16[512]{0:T(512)(128)(2,1)S(1)}, bf16[512]{0:T(512)(128)(2,1)}, u32[]{:S(2)}) copy-start(bf16[512]{0:T(512)(128)(2,1)} %get-tuple-element.73) | copy-start | bytes 3076
  139.3 28.4 %copy-start.158 = (bf16[512]{0:T(512)(128)(2,1)S(1)}, bf16[512]{0:T(512)(128)(2,1)}, u32[]{:S(2)}) copy-start(bf16[512]{0:T(512)(128)(2,1)} %get-tuple-element.74) | copy-start | bytes 3076
  139.4 28.5 %copy-start.157 = (bf16[512]{0:T(512)(128)(2,1)S(1)}, bf16[512]{0:T(512)(128)(2,1)}, u32[]{:S(2)}) copy-start(bf16[512]{0:T(512)(128)(2,1)} %get-tuple-element.75) | copy-start | bytes 3076
  139.4 28.6 %copy-start.156 = (bf16[512]{0:T(512)(128)(2,1)S(1)}, bf16[512]{0:T(512)(128)(2,1)}, u32[]{:S(2)}) copy-start(bf16[512]{0:T(512)(128)(2,1)} %get-tuple-element.76) | copy-start | bytes 3076
  139.4 28.7 %copy-start.155 = (bf16[512]{0:T(512)(128)(2,1)S(1)}, bf16[512]{0:T(512)(128)(2,1)}, u32[]{:S(2)}) copy-start(bf16[512]{0:T(512)(128)(2,1)} %get-tuple-element.77) | copy-start | bytes 3076
  139.4 28.7 %copy-start.154 = (bf16[512]{0:T(512)(128)(2,1)S(1)}, bf16[512]{0:T(512)(128)(2,1)}, u32[]{:S(2)}) copy-start(bf16[512]{0:T(512)(128)(2,1)} %get-tuple-element.78) | copy-start | bytes 3076
  139.4 28.8 %copy-start.153 = (bf16[512]{0:T(512)(128)(2,1)S(1)}, bf16[512]{0:T(512)(128)(2,1)}, u32[]{:S(2)}) copy-start(bf16[512]{0:T(512)(128)(2,1)} %get-tuple-element.79) | copy-start | bytes 3076
  139.4 28.9 %copy-start.150 = (bf16[512]{0:T(512)(128)(2,1)S(1)}, bf16[512]{0:T(512)(128)(2,1)}, u32[]{:S(2)}) copy-start(bf16[512]{0:T(512)(128)(2,1)} %get-tuple-element.81) | copy-start | bytes 3076
  139.4 29.0 %copy-start.149 = (bf16[512]{0:T(512)(128)(2,1)S(1)}, bf16[512]{0:T(512)(128)(2,1)}, u32[]{:S(2)}) copy-start(bf16[512]{0:T(512)(128)(2,1)} %get-tuple-element.82) | copy-start | bytes 3076
  139.4 29.0 %copy-start.148 = (bf16[512]{0:T(512)(128)(2,1)S(1)}, bf16[512]{0:T(512)(128)(2,1)}, u32[]{:S(2)}) copy-start(bf16[512]{0:T(512)(128)(2,1)} %get-tuple-element.80) | copy-start | bytes 3076
  139.4 29.1 %copy-start.152 = (bf16[512]{0:T(512)(128)(2,1)S(1)}, bf16[512]{0:T(512)(128)(2,1)}, u32[]{:S(2)}) copy-start(bf16[512]{0:T(512)(128)(2,1)} %get-tuple-element.62) | copy-start | bytes 3076
  139.4 29.2 %copy-start.146 = (bf16[512]{0:T(512)(128)(2,1)S(1)}, bf16[512]{0:T(512)(128)(2,1)}, u32[]{:S(2)}) copy-start(bf16[512]{0:T(512)(128)(2,1)} %get-tuple-element.188) | copy-start | bytes 3076
  139.5 30.8 %copy-start.145 = (bf16[512]{0:T(512)(128)(2,1)S(1)}, bf16[512]{0:T(512)(128)(2,1)}, u32[]{:S(2)}) copy-start(bf16[512]{0:T(512)(128)(2,1)} %get-tuple-element.186) | copy-start | bytes 3076
  139.5 32.4 %copy-start.75 = (bf16[1,8,64]{2,0,1:T(2,128)(2,1)S(1)}, bf16[1,8,64]{2,0,1:T(2,128)(2,1)}, u32[]{:S(2)}) copy-start(bf16[1,8,64]{2,0,1:T(2,128)(2,1)} %concatenate.718) | copy-start | bytes 3076
  139.5 32.4 %copy-start.76 = (bf16[1,8,64]{2,0,1:T(2,128)(2,1)S(1)}, bf16[1,8,64]{2,0,1:T(2,128)(2,1)}, u32[]{:S(2)}) copy-start(bf16[1,8,64]{2,0,1:T(2,128)(2,1)} %concatenate.719) | copy-start | bytes 3076
  139.5 32.4 %copy-start.77 = (bf16[1,8,64]{2,0,1:T(2,128)(2,1)S(1)}, bf16[1,8,64]{2,0,1:T(2,128)(2,1)}, u32[]{:S(2)}) copy-start(bf16[1,8,64]{2,0,1:T(2,128)(2,1)} %concatenate.720) | copy-start | bytes 3076
  139.5 32.4 %copy-start.78 = (bf16[1,8,64]{2,0,1:T(2,128)(2,1)S(1)}, bf16[1,8,64]{2,0,1:T(2,128)(2,1)}, u32[]{:S(2)}) copy-start(bf16[1,8,64]{2,0,1:T(2,128)(2,1)} %concatenate.721) | copy-start | bytes 3076
  139.5 32.4 %copy-start.79 = (bf16[1,8,64]{2,0,1:T(2,128)(2,1)S(1)}, bf16[1,8,64]{2,0,1:T(2,128)(2,1)}, u32[]{:S(2)}) copy-start(bf16[1,8,64]{2,0,1:T(2,128)(2,1)} %concatenate.722) | copy-start | bytes 3076
  139.5 32.4 %copy-start.80 = (bf16[1,8,64]{2,0,1:T(2,128)(2,1)S(1)}, bf16[1,8,64]{2,0,1:T(2,128)(2,1)}, u32[]{:S(2)}) copy-start(bf16[1,8,64]{2,0,1:T(2,128)(2,1)} %concatenate.723) | copy-start | bytes 3076
  139.5 32.4 %copy-start.81 = (bf16[1,8,64]{2,0,1:T(2,128)(2,1)S(1)}, bf16[1,8,64]{2,0,1:T(2,128)(2,1)}, u32[]{:S(2)}) copy-start(bf16[1,8,64]{2,0,1:T(2,128)(2,1)} %concatenate.724) | copy-start | bytes 3076
  139.5 32.4 %copy-start.82 = (bf16[1,8,64]{2,0,1:T(2,128)(2,1)S(1)}, bf16[1,8,64]{2,0,1:T(2,128)(2,1)}, u32[]{:S(2)}) copy-start(bf16[1,8,64]{2,0,1:T(2,128)(2,1)} %concatenate.725) | copy-start | bytes 3076
  139.6 32.4 %copy-start.83 = (bf16[1,8,64]{2,0,1:T(2,128)(2,1)S(1)}, bf16[1,8,64]{2,0,1:T(2,128)(2,1)}, u32[]{:S(2)}) copy-start(bf16[1,8,64]{2,0,1:T(2,128)(2,1)} %concatenate.726) | copy-start | bytes 3076
  139.6 32.4 %copy-start.84 = (bf16[1,8,64]{2,0,1:T(2,128)(2,1)S(1)}, bf16[1,8,64]{2,0,1:T(2,128)(2,1)}, u32[]{:S(2)}) copy-start(bf16[1,8,64]{2,0,1:T(2,128)(2,1)} %concatenate.727) | copy-start | bytes 3076
  139.6 32.4 %copy-start.85 = (bf16[1,8,64]{2,0,1:T(2,128)(2,1)S(1)}, bf16[1,8,64]{2,0,1:T(2,128)(2,1)}, u32[]{:S(2)}) copy-start(bf16[1,8,64]{2,0,1:T(2,128)(2,1)} %concatenate.728) | copy-start | bytes 3076
  139.6 32.4 %copy-start.86 = (bf16[1,8,64]{2,0,1:T(2,128)(2,1)S(1)}, bf16[1,8,64]{2,0,1:T(2,128)(2,1)}, u32[]{:S(2)}) copy-start(bf16[1,8,64]{2,0,1:T(2,128)(2,1)} %concatenate.729) | copy-start | bytes 3076
  139.6 32.4 %copy-start.87 = (bf16[1,8,64]{2,0,1:T(2,128)(2,1)S(1)}, bf16[1,8,64]{2,0,1:T(2,128)(2,1)}, u32[]{:S(2)}) copy-start(bf16[1,8,64]{2,0,1:T(2,128)(2,1)} %concatenate.730) | copy-start | bytes 3076
  139.6 32.4 %copy-start.88 = (bf16[1,8,64]{2,0,1:T(2,128)(2,1)S(1)}, bf16[1,8,64]{2,0,1:T(2,128)(2,1)}, u32[]{:S(2)}) copy-start(bf16[1,8,64]{2,0,1:T(2,128)(2,1)} %concatenate.731) | copy-start | bytes 3076
  139.6 32.4 %copy-start.89 = (bf16[1,8,64]{2,0,1:T(2,128)(2,1)S(1)}, bf16[1,8,64]{2,0,1:T(2,128)(2,1)}, u32[]{:S(2)}) copy-start(bf16[1,8,64]{2,0,1:T(2,128)(2,1)} %concatenate.732) | copy-start | bytes 3076
  139.6 32.4 %copy-start.90 = (bf16[1,8,64]{2,0,1:T(2,128)(2,1)S(1)}, bf16[1,8,64]{2,0,1:T(2,128)(2,1)}, u32[]{:S(2)}) copy-start(bf16[1,8,64]{2,0,1:T(2,128)(2,1)} %concatenate.733) | copy-start | bytes 3076
  139.6 32.4 %copy-start.91 = (bf16[1,8,64]{2,0,1:T(2,128)(2,1)S(1)}, bf16[1,8,64]{2,0,1:T(2,128)(2,1)}, u32[]{:S(2)}) copy-start(bf16[1,8,64]{2,0,1:T(2,128)(2,1)} %concatenate.734) | copy-start | bytes 3076
  139.6 32.4 %copy-start.92 = (bf16[1,8,64]{2,0,1:T(2,128)(2,1)S(1)}, bf16[1,8,64]{2,0,1:T(2,128)(2,1)}, u32[]{:S(2)}) copy-start(bf16[1,8,64]{2,0,1:T(2,128)(2,1)} %concatenate.735) | copy-start | bytes 3076
  139.7 32.4 %copy-start.93 = (bf16[1,8,64]{2,0,1:T(2,128)(2,1)S(1)}, bf16[1,8,64]{2,0,1:T(2,128)(2,1)}, u32[]{:S(2)}) copy-start(bf16[1,8,64]{2,0,1:T(2,128)(2,1)} %concatenate.736) | copy-start | bytes 3076
  139.7 32.4 %copy-start.94 = (bf16[1,8,64]{2,0,1:T(2,128)(2,1)S(1)}, bf16[1,8,64]{2,0,1:T(2,128)(2,1)}, u32[]{:S(2)}) copy-start(bf16[1,8,64]{2,0,1:T(2,128)(2,1)} %concatenate.737) | copy-start | bytes 3076
  139.7 32.4 %copy-start.95 = (bf16[1,8,64]{2,0,1:T(2,128)(2,1)S(1)}, bf16[1,8,64]{2,0,1:T(2,128)(2,1)}, u32[]{:S(2)}) copy-start(bf16[1,8,64]{2,0,1:T(2,128)(2,1)} %concatenate.738) | copy-start | bytes 3076
  139.7 32.4 %copy-start.96 = (bf16[1,8,64]{2,0,1:T(2,128)(2,1)S(1)}, bf16[1,8,64]{2,0,1:T(2,128)(2,1)}, u32[]{:S(2)}) copy-start(bf16[1,8,64]{2,0,1:T(2,128)(2,1)} %concatenate.739) | copy-start | bytes 3076
  139.7 32.4 %copy-start.97 = (bf16[1,8,64]{2,0,1:T(2,128)(2,1)S(1)}, bf16[1,8,64]{2,0,1:T(2,128)(2,1)}, u32[]{:S(2)}) copy-start(bf16[1,8,64]{2,0,1:T(2,128)(2,1)} %concatenate.740) | copy-start | bytes 3076
  139.7 32.4 %copy-start.98 = (bf16[1,8,64]{2,0,1:T(2,128)(2,1)S(1)}, bf16[1,8,64]{2,0,1:T(2,128)(2,1)}, u32[]{:S(2)}) copy-start(bf16[1,8,64]{2,0,1:T(2,128)(2,1)} %concatenate.741) | copy-start | bytes 3076
  163.0 11.1 %copy-start.6 = (bf16[8,16,512]{2,1,0:T(8,128)(2,1)S(1)}, bf16[8,16,512]{2,1,0:T(8,128)(2,1)}, u32[]{:S(2)}) copy-start(bf16[8,16,512]{2,1,0:T(8,128)(2,1)} %copy-done.5) | copy-start | bytes 393220
  178.8 74.6 %copy-start.2 = (bf16[1,8,16,512]{3,2,1,0:T(8,128)(2,1)S(1)}, bf16[1,8,16,512]{3,2,1,0:T(8,128)(2,1)}, u32[]{:S(2)}) copy-start(bf16[1,8,16,512]{3,2,1,0:T(8,128)(2,1)} %get-tuple-element.198) | copy-start | bytes 393220
  (147 other events, 919.7 us)
Sparse Core Ops, SparseCore 0:
  9.5 16.3 all-gather.4
  27.5 14.8 all-gather.6
